TPU v7x, 32 devices: a whole 2x2x4 slice. The times are simulated.
32 devices in a mesh: tok: 16 (over z, x, core), lyr: 2 (over y).
Axes of the slice: x: 2, y: 2, z: 4, core: 2. Of those that a mesh axis runs over, the one named last changes fastest.
Arguments:
- feature_codes: bfloat16 [4, 2048, 2, 256], P('lyr', 'tok'), may hold values from 0 to 21, as said below
- block_ids: int32 [4, 2048, 2], P('lyr', 'tok'), may hold values from 0 to 31, all different within a row; in each aligned block of 128 rows (0 to 127, 128 to 255, ..., all dimensions but the last counted through in order) at most 16 rows name the same one
- target_layer: int32 [2048], P('tok'), may hold values from 0 to 3
- request_ids: int32 [2048], P('tok'), may hold values from 0 to 15
- target_resid: bfloat16 [2048, 2304], P('tok'), may hold values from -6 to 6
- decoder: bfloat16 [4, 8192, 2304], P('lyr', 'tok'), may hold values from -0.25 to 0.25
Outputs:
- scores: bfloat16 [4, 2048, 2, 256], P('lyr', 'tok')
- request_totals: float32 [16, 4, 8192], P(None, 'lyr', 'tok')
Inputs may be any that keep to these rules, and one draw needn't show every extreme that they name: `block_ids`: the 2 panel indices of one token at one source layer are distinct; among the 128 tokens of one index of tok at one source layer no panel is named by more than 16 of them, a bound that some block reaches. `feature_codes`: nonnegative, with many entries zero.
All inputs are finite; a program needn't handle non-finite values.
Results may differ from a plain program's by a relative error of at most 0.0053.
Values may be sent and summed in bfloat16 or wider, within the bound.
A program may use at most 64 MiB of HBM per device.

v0:
```python
import jax
import jax.numpy as jnp
from jax import lax
from jax.sharding import PartitionSpec as P

PANELS = 32
REQUESTS = 16
CAP = 16


def slot_of(flat_ids):
    one_hot = (flat_ids[:, None] == jnp.arange(PANELS, dtype=jnp.int32)[None, :]).astype(jnp.int32)
    before = jnp.cumsum(one_hot, axis=0) - one_hot
    return flat_ids * CAP + jnp.sum(before * one_hot, axis=1)


def source_of(slot_ids):
    row_count = slot_ids.shape[0]
    empty = jnp.full((PANELS * CAP,), row_count, jnp.int32)
    return empty.at[slot_ids].set(jnp.arange(row_count, dtype=jnp.int32))


def take_rows(table, index):
    return jnp.take(table, index, axis=0)


def pad_zero(table):
    return jnp.concatenate([table, jnp.zeros((1,) + table.shape[1:], table.dtype)], axis=0)


def normalize_error(resid_rows, rebuilt):
    error = resid_rows.astype(jnp.float32) - rebuilt
    spread = jnp.mean(error * error, axis=-1, keepdims=True)
    return (error * lax.rsqrt(spread + 1e-06)).astype(jnp.bfloat16)


def per_device(feature_codes, block_ids, target_layer, request_ids, target_resid, decoder):
    layers_here, count, kact, panel = feature_codes.shape
    width = target_resid.shape[1]
    tok_count = lax.axis_size("tok")
    per_dev = PANELS // tok_count
    rows_here = count * kact
    first_layer = lax.axis_index("lyr") * layers_here
    layer_ids = first_layer + jnp.arange(layers_here, dtype=jnp.int32)
    alive_mask = (layer_ids[:, None] <= target_layer[None, :]).astype(feature_codes.dtype)
    masked = feature_codes * alive_mask[:, :, None, None]
    flat_ids = block_ids.reshape(layers_here, rows_here)
    slot_ids = jax.vmap(slot_of)(flat_ids)
    source_rows = jax.vmap(source_of)(slot_ids)
    token_of = source_rows // kact
    code_rows = jax.vmap(pad_zero)(masked.reshape(layers_here, rows_here, panel))
    send_codes = jax.vmap(take_rows)(code_rows, source_rows).reshape(
        layers_here, tok_count, per_dev, CAP, panel
    )
    panel_weights = decoder.reshape(layers_here, per_dev, panel, width)
    slot_requests = jnp.take(pad_zero(request_ids), token_of, axis=0).reshape(
        layers_here, tok_count, per_dev, CAP
    )
    received, request_slots = (
        lax.all_to_all(send_codes, "tok", split_axis=1, concat_axis=1, tiled=True),
        lax.all_to_all(slot_requests, "tok", split_axis=1, concat_axis=1, tiled=True),
    )
    built = jnp.einsum(
        "lspcj,lpjd->lspcd", received, panel_weights, preferred_element_type=jnp.float32
    ).astype(jnp.bfloat16)
    returned = lax.all_to_all(built, "tok", split_axis=1, concat_axis=1, tiled=True).reshape(
        layers_here, PANELS * CAP, width
    )
    per_row = jax.vmap(take_rows)(returned, slot_ids)
    partial_value = jnp.sum(
        per_row.astype(jnp.float32).reshape(layers_here, count, kact, width), axis=(0, 2)
    )
    rebuilt = lax.psum(partial_value, "lyr")
    gradient = normalize_error(target_resid, rebuilt)
    send_grad = jnp.take(pad_zero(gradient), token_of, axis=0).reshape(
        layers_here, tok_count, per_dev, CAP, width
    )
    received_grad = lax.all_to_all(send_grad, "tok", split_axis=1, concat_axis=1, tiled=True)
    projected_slots = jnp.einsum(
        "lspcd,lpjd->lspcj", received_grad, panel_weights, preferred_element_type=jnp.float32
    ).astype(jnp.bfloat16)
    coming_back = lax.all_to_all(
        projected_slots, "tok", split_axis=1, concat_axis=1, tiled=True
    ).reshape(layers_here, PANELS * CAP, panel)
    picked = jax.vmap(take_rows)(coming_back, slot_ids).reshape(layers_here, count, kact, panel)
    attribution_rows = masked.astype(jnp.float32) * picked.astype(jnp.float32)
    scores = attribution_rows.astype(jnp.bfloat16)
    attribution = received.astype(jnp.float32) * projected_slots.astype(jnp.float32)
    members = (request_slots[..., None] == jnp.arange(REQUESTS, dtype=jnp.int32)).astype(
        jnp.float32
    )
    owned = jnp.einsum("lspcr,lspcj->rlpj", members, attribution, precision=lax.Precision.HIGHEST)
    request_totals = owned.reshape(REQUESTS, layers_here, per_dev * panel)
    return (scores, request_totals)


def solution(mesh):
    placed = (
        P("lyr", "tok", None, None),
        P("lyr", "tok", None),
        P("tok"),
        P("tok"),
        P("tok", None),
        P("lyr", "tok", None),
    )
    return jax.shard_map(
        per_device,
        mesh=mesh,
        in_specs=placed,
        out_specs=(P("lyr", "tok", None, None), P(None, "lyr", "tok")),
        check_vma=False,
    )
```

profile of v0, /device:TPU:0, one launch (start us, length us, event | category | flops | bytes accessed | tf_op | source)
XLA Modules:
  0.0 417.4 jit_solution(11479595752540939134)
XLA Ops:
  7.2 0.9 copy.84
  9.0 1.2 reduce-window.6
  10.9 24.5 %scatter_fusion = s32[2,512]{1,0:T(2,128)S(1)} fusion(s32[2,512]{1,0:T(2,128)S(1)} %broadcast_in_dim.71, s32[512]{0:T(512)S(1)} %bitcast.74, s32[512]{0:T(512)S(1)} %bitcast.84), kind=kCustom, calls=%fused_computation.5 | custom fusion | bytes 10240 | tf_op jit(solution)/shard_map/vmap()/scatter | solution.py:20
  36.7 5.5 %gather_fusion.2 = bf16[1024,256]{1,0:T(8,128)(2,1)S(1)} fusion(bf16[2,257,256]{2,0,1:T(2,128)(2,1)S(1)} %concatenate.9, s32[1024]{0:T(1024)S(1)} %bitcast.73), kind=kCustom, calls=%fused_computation.2 | custom fusion | bytes 1056768 | tf_op jit(solution)/shard_map/vmap(jit(_take))/gather | solution.py:24
  42.4 21.5 %all_to_all.25 = bf16[2,16,2,16,256]{4,3,2,0,1:T(8,128)(2,1)S(1)} all-to-all(bf16[2,16,2,16,256]{4,3,2,0,1:T(8,128)(2,1)S(1)} %copy.91), channel_id=1, replica_groups=mesh['tok'=16,'lyr'=2] {'tok'}, dimensions={1} | all-to-all | bytes 1048576 | tf_op jit(solution)/shard_map/all_to_all | solution.py:60
  63.9 3.7 fusion
  67.6 2.7 copy.93
  70.3 4.6 %all-to-all-start.1 = ((bf16[2,16,2,16,2304]{4,3,2,0,1:T(8,128)(2,1)}), bf16[2,16,2,16,2304]{4,3,2,0,1:T(8,128)(2,1)}, u32[]{:S(2)}, u32[]{:S(2)}) async-start(bf16[2,16,2,16,2304]{4,3,2,0,1:T(8,128)(2,1)} %copy.93), calls=%async_computation.1 | async-start | bytes 9437184 | tf_op jit(solution)/shard_map/all_to_all | solution.py:66
  75.2 86.4 %all-to-all-done.1 = bf16[2,16,2,16,2304]{4,3,2,0,1:T(8,128)(2,1)} async-done(((bf16[2,16,2,16,2304]{4,3,2,0,1:T(8,128)(2,1)}), bf16[2,16,2,16,2304]{4,3,2,0,1:T(8,128)(2,1)}, u32[]{:S(2)}, u32[]{:S(2)}) %all-to-all-start.1) | async-done | bytes 4718624 | tf_op jit(solution)/shard_map/all_to_all | solution.py:66
  161.5 4.9 %copy.94 = bf16[2,16,2,16,2304]{4,3,2,1,0:T(8,128)(2,1)} copy(bf16[2,16,2,16,2304]{4,3,2,0,1:T(8,128)(2,1)} %all-to-all-done.1) | data formatting | bytes 9437184 | tf_op jit(solution)/shard_map/all_to_all | solution.py:66
  166.4 13.5 %gather_fusion.3 = bf16[512,2304]{1,0:T(8,128)(2,1)} fusion(bf16[2,512,2304]{2,1,0:T(8,128)(2,1)} %bitcast.72, s32[512]{0:T(512)S(1)} %bitcast.70), kind=kCustom, calls=%fused_computation.3 | custom fusion | bytes 4722688 | tf_op jit(solution)/shard_map/vmap(jit(_take))/gather | solution.py:24
  179.9 2.4 convert_reduce_fusion
  182.2 2.5 reduce_sum.42
  184.7 5.5 %reduce_sum.43 = f32[128,2304]{1,0:T(8,128)} reduce(f32[128,2,2304]{2,1,0:T(2,128)} %reduce_sum.42, f32[]{:T(128)} %constant.104.clone.1), dimensions={1}, to_apply=%region_5.6 | reduce | flops 294912 | bytes 3538948 | tf_op jit(solution)/shard_map/reduce_sum | solution.py:70
  190.3 60.2 %all-reduce.4.cloned.1.call-done = f32[128,2304]{1,0:T(8,128)} async-done(((f32[128,2304]{1,0:T(8,128)}), f32[128,2304]{1,0:T(8,128)}) %all-reduce.4.cloned.1.call-update) | async-done | bytes 1179664 | tf_op jit(solution)/shard_map/psum | solution.py:73
  250.5 1.5 multiply_reduce_fusion
  252.1 1.5 multiply_convert_fusion
  253.6 6.2 %gather_fusion = bf16[1024,2304]{1,0:T(8,128)(2,1)} fusion(bf16[129,2304]{1,0:T(8,128)(2,1)S(1)} %concatenate.10, s32[1024]{0:T(1024)S(1)} %broadcast_clamp_fusion), kind=kCustom, calls=%fused_computation | custom fusion | bytes 9441280 | tf_op jit(solution)/shard_map/jit(_take)/gather | solution.py:75
  259.8 2.8 broadcast_select_fusion
  262.6 2.6 copy.96
  265.2 5.8 %all-to-all-start.2 = ((bf16[2,16,2,16,2304]{4,3,2,0,1:T(8,128)(2,1)}), bf16[2,16,2,16,2304]{4,3,2,0,1:T(8,128)(2,1)}, u32[]{:S(2)}, u32[]{:S(2)}) async-start(bf16[2,16,2,16,2304]{4,3,2,0,1:T(8,128)(2,1)} %copy.96), calls=%async_computation.2 | async-start | bytes 9437184 | tf_op jit(solution)/shard_map/all_to_all | solution.py:78
  271.0 6.9 %gather_fusion.1 = s32[1024]{0:T(1024)S(1)} fusion(s32[129]{0:T(256)S(1)} %pad_add_fusion, s32[1024]{0:T(1024)S(1)} %broadcast_clamp_fusion), kind=kCustom, calls=%fused_computation.1 | custom fusion | bytes 12288 | tf_op jit(solution)/shard_map/jit(_take)/gather | solution.py:56
  278.7 79.0 %all-to-all-done.2 = bf16[2,16,2,16,2304]{4,3,2,0,1:T(8,128)(2,1)} async-done(((bf16[2,16,2,16,2304]{4,3,2,0,1:T(8,128)(2,1)}), bf16[2,16,2,16,2304]{4,3,2,0,1:T(8,128)(2,1)}, u32[]{:S(2)}, u32[]{:S(2)}) %all-to-all-start.2) | async-done | bytes 4718624 | tf_op jit(solution)/shard_map/all_to_all | solution.py:78
  357.7 21.7 %all-to-all-start.4 = ((s32[2,16,2,16]{3,2,0,1:T(2,128)}), s32[2,16,2,16]{3,2,0,1:T(2,128)S(1)}, u32[]{:S(2)}, u32[]{:S(2)}) async-start(s32[2,16,2,16]{3,2,0,1:T(2,128)} %copy.101), calls=%async_computation.4 | async-start | bytes 65536 | tf_op jit(solution)/shard_map/all_to_all | solution.py:61
  379.4 5.2 %fusion.6 = bf16[2,16,2,16,256]{4,3,1,2,0:T(8,128)(2,1)S(1)} fusion(bf16[2,2,256,2304,1]{3,2,4,1,0:T(8,128)(2,1)} %bitcast.79, bf16[2,16,2,16,2304]{4,3,2,0,1:T(8,128)(2,1)} %all-to-all-done.2), kind=kOutput, calls=%fused_computation.13 | convolution fusion | flops 1208221696 | bytes 9961472 | tf_op jit(solution)/shard_map/lspcd,lpjd->lspcj/dot_general | solution.py:79
  384.7 0.9 copy.98
  386.1 5.5 %all-to-all-start.3 = ((bf16[2,16,2,16,256]{4,3,2,0,1:T(8,128)(2,1)}), bf16[2,16,2,16,256]{4,3,2,0,1:T(8,128)(2,1)S(1)}, u32[]{:S(2)}, u32[]{:S(2)}) async-start(bf16[2,16,2,16,256]{4,3,2,0,1:T(8,128)(2,1)} %copy.98), calls=%async_computation.3 | async-start | bytes 1048576 | tf_op jit(solution)/shard_map/all_to_all | solution.py:82
  392.0 0.7 convolution_bitcast_fusion
  392.7 0.7 reshape.203
  393.4 12.4 %all-to-all-done.3 = bf16[2,16,2,16,256]{4,3,2,0,1:T(8,128)(2,1)S(1)} async-done(((bf16[2,16,2,16,256]{4,3,2,0,1:T(8,128)(2,1)}), bf16[2,16,2,16,256]{4,3,2,0,1:T(8,128)(2,1)S(1)}, u32[]{:S(2)}, u32[]{:S(2)}) %all-to-all-start.3) | async-done | bytes 524320 | tf_op jit(solution)/shard_map/all_to_all | solution.py:82
  405.8 3.2 gather_fusion.4
  409.1 1.4 multiply_convert_fusion.1
  (60 shorter events, 5.4 us)
Async XLA Ops:
  7.2 28.4 %copy-start.5 = (s32[128]{0:T(128)S(1)}, s32[128]{0:T(128)}, u32[]{:S(2)}) copy-start(s32[128]{0:T(128)} %param.8) | copy-start | bytes 1540
  7.2 28.5 %copy-start.1 = (bf16[2,128,2,256]{3,2,1,0:T(2,128)(2,1)S(1)}, bf16[2,128,2,256]{3,2,1,0:T(2,128)(2,1)}, u32[]{:S(2)}) copy-start(bf16[2,128,2,256]{3,2,1,0:T(2,128)(2,1)} %param.6) | copy-start | bytes 786436
  70.3 91.2 %all-to-all-start.1 = ((bf16[2,16,2,16,2304]{4,3,2,0,1:T(8,128)(2,1)}), bf16[2,16,2,16,2304]{4,3,2,0,1:T(8,128)(2,1)}, u32[]{:S(2)}, u32[]{:S(2)}) async-start(bf16[2,16,2,16,2304]{4,3,2,0,1:T(8,128)(2,1)} %copy.93), calls=%async_computation.1 | async-start | bytes 9437184 | tf_op jit(solution)/shard_map/all_to_all | solution.py:66
  74.9 175.6 %all-reduce.4.cloned.1.call-start = ((), (), s32[]{:S(2)}) async-start(), calls=%async_computation.5 | async-start | bytes 2359296 | tf_op jit(solution)/shard_map/psum | solution.py:73
  182.2 68.3 %copy-start = (bf16[128,2304]{1,0:T(8,128)(2,1)S(1)}, bf16[128,2304]{1,0:T(8,128)(2,1)}, u32[]{:S(2)}) copy-start(bf16[128,2304]{1,0:T(8,128)(2,1)} %param.10) | copy-start | bytes 1769476
  265.2 5.8 %copy-start.4 = (s32[128]{0:T(128)S(1)}, s32[128]{0:T(128)}, u32[]{:S(2)}) copy-start(s32[128]{0:T(128)} %param.9) | copy-start | bytes 1540
  265.2 92.5 %all-to-all-start.2 = ((bf16[2,16,2,16,2304]{4,3,2,0,1:T(8,128)(2,1)}), bf16[2,16,2,16,2304]{4,3,2,0,1:T(8,128)(2,1)}, u32[]{:S(2)}, u32[]{:S(2)}) async-start(bf16[2,16,2,16,2304]{4,3,2,0,1:T(8,128)(2,1)} %copy.96), calls=%async_computation.2 | async-start | bytes 9437184 | tf_op jit(solution)/shard_map/all_to_all | solution.py:78
  357.7 28.4 %all-to-all-start.4 = ((s32[2,16,2,16]{3,2,0,1:T(2,128)}), s32[2,16,2,16]{3,2,0,1:T(2,128)S(1)}, u32[]{:S(2)}, u32[]{:S(2)}) async-start(s32[2,16,2,16]{3,2,0,1:T(2,128)} %copy.101), calls=%async_computation.4 | async-start | bytes 65536 | tf_op jit(solution)/shard_map/all_to_all | solution.py:61
  379.4 12.3 %copy-start.3 = (s32[2,128,2]{1,2,0:T(2,128)S(1)}, s32[2,128,2]{1,2,0:T(2,128)}, u32[]{:S(2)}) copy-start(s32[2,128,2]{1,2,0:T(2,128)} %param.7) | copy-start | bytes 6148
  384.6 24.5 %copy-start.2 = (bf16[2,128,2,256]{3,2,1,0:T(2,128)(2,1)S(1)}, bf16[2,128,2,256]{3,2,1,0:T(2,128)(2,1)}, u32[]{:S(2)}) copy-start(bf16[2,128,2,256]{3,2,1,0:T(2,128)(2,1)} %param.6) | copy-start | bytes 786436
  386.1 19.7 %all-to-all-start.3 = ((bf16[2,16,2,16,256]{4,3,2,0,1:T(8,128)(2,1)}), bf16[2,16,2,16,256]{4,3,2,0,1:T(8,128)(2,1)S(1)}, u32[]{:S(2)}, u32[]{:S(2)}) async-start(bf16[2,16,2,16,256]{4,3,2,0,1:T(8,128)(2,1)} %copy.98), calls=%async_computation.3 | async-start | bytes 1048576 | tf_op jit(solution)/shard_map/all_to_all | solution.py:82
Sparse Core Ops, SparseCore 0:
  190.3 60.1 all-reduce.3
where the time goes:
time: 418 us; the launch traced here: 417 us
  waiting for transfers between devices  238 us (57%)
  local copies, waits for them, and re-layouts  77.8 us (19%)
  starting transfers between devices  37.8 us (9%)
  blocking collectives  21.5 us (5%)
  other arithmetic  17.8 us (4%)
  between operations  14.4 us (3%)
  matrix products  9.62 us (2%)
    all_to_all x1, waiting for transfers between devices, per_device(): lax.all_to_all(built, 'tok', split_axis=1, concat_axis=1, tiled=True)  86.4 us
    all_to_all x1, waiting for transfers between devices, per_device(): lax.all_to_all(send_grad, 'tok', split_axis=1, concat_axis=1, tiled=True)  79 us
    psum x1, waiting for transfers between devices, per_device(): rebuilt = lax.psum(partial_value, 'lyr')  60.2 us
    scatter x1, local copies, waits for them, and re-layouts, source_of(): return empty.at[slot_ids].set(jnp.arange(row_count, dtype=jnp.int32))  24.5 us
    gather x4, local copies, waits for them, and re-layouts, take_rows(): return jnp.take(table, index, axis=0)  22.2 us
    all_to_all x1, starting transfers between devices, per_device(): lax.all_to_all(slot_requests, 'tok', split_axis=1, concat_axis=1, tiled=T...  21.7 us
    all_to_all x1, blocking collectives, per_device(): lax.all_to_all(send_codes, 'tok', split_axis=1, concat_axis=1, tiled=True)  21.5 us
    all_to_all x1, waiting for transfers between devices, per_device(): lax.all_to_all(projected_slots, 'tok', split_axis=1, concat_axis=1, tiled...  12.4 us
  transfers between devices with their start and end apart: 5, of which 5 were waited for; matrix products, arithmetic and copies ran while one was open for 4% of the time, Pallas kernels for 0%

commit v1 on v0

v1 whole, which is shorter than its diff:
```python
import jax
import jax.numpy as jnp
from jax import lax
from jax.sharding import PartitionSpec as P

REQUESTS = 16


def per_device(feature_codes, block_ids, target_layer, request_ids, target_resid, decoder):
    layers_here, count, kact, panel = feature_codes.shape
    width = target_resid.shape[1]
    features = decoder.shape[1]
    per_dev = features // panel
    tok, lyr = lax.axis_index("tok"), lax.axis_index("lyr")
    lyr_count = lax.axis_size("lyr")
    layer_ids = lyr * layers_here + jnp.arange(layers_here, dtype=jnp.int32)
    alive = layer_ids[:, None] <= target_layer[None, :]
    masked = jnp.where(alive[:, :, None, None], feature_codes, jnp.zeros_like(feature_codes))
    all_codes = lax.all_gather(masked, "tok", axis=1, tiled=True)
    all_ids = lax.all_gather(block_ids, "tok", axis=1, tiled=True)
    all_requests = lax.all_gather(request_ids, "tok", axis=0, tiled=True)
    mine = tok * per_dev + jnp.arange(per_dev, dtype=jnp.int32)
    named = (all_ids[..., None] == mine).astype(jnp.bfloat16)
    dense = jnp.sum(all_codes[:, :, :, None, :] * named[..., None], axis=2)
    tokens = dense.shape[1]
    dense = jnp.swapaxes(dense, 0, 1).reshape(tokens, layers_here * features)
    weights = decoder.reshape(layers_here * features, width)
    partial = jnp.dot(dense, weights, preferred_element_type=jnp.float32).astype(jnp.bfloat16)
    rebuilt = lax.psum_scatter(partial, ("tok", "lyr"), scatter_dimension=0, tiled=True)
    rows = count // lyr_count
    resid = lax.dynamic_slice_in_dim(target_resid, lyr * rows, rows, 0)
    error = resid.astype(jnp.float32) - rebuilt.astype(jnp.float32)
    spread = jnp.mean(error * error, axis=-1, keepdims=True)
    gradient = (error * lax.rsqrt(spread + 1e-06)).astype(jnp.bfloat16)
    gradients = lax.all_gather(gradient, ("tok", "lyr"), axis=0, tiled=True)
    projected = lax.dot_general(
        gradients, weights, (((1,), (1,)), ((), ())), preferred_element_type=jnp.float32
    ).astype(jnp.bfloat16)
    attribution = dense.astype(jnp.float32) * projected.astype(jnp.float32)
    members = (all_requests[:, None] == jnp.arange(REQUESTS, dtype=jnp.int32)).astype(jnp.float32)
    totals = lax.dot_general(
        members, attribution, (((0,), (0,)), ((), ())), precision=lax.Precision.HIGHEST
    ).reshape(REQUESTS, layers_here, features)
    scored = attribution.astype(jnp.bfloat16).reshape(tokens, layers_here, 1, per_dev, panel)
    spread_out = jnp.sum(
        scored * jnp.swapaxes(named, 0, 1)[..., None], axis=3
    )
    scores = lax.psum_scatter(
        jnp.swapaxes(spread_out, 0, 1), "tok", scatter_dimension=1, tiled=True
    )
    return (scores, totals)


def solution(mesh):
    placed = (
        P("lyr", "tok", None, None),
        P("lyr", "tok", None),
        P("tok"),
        P("tok"),
        P("tok", None),
        P("lyr", "tok", None),
    )
    return jax.shard_map(
        per_device,
        mesh=mesh,
        in_specs=placed,
        out_specs=(P("lyr", "tok", None, None), P(None, "lyr", "tok")),
        check_vma=False,
    )
```

time: 418 us -> 449 us (1.074)
  waiting for transfers between devices: 238 us -> 289 us
  starting transfers between devices: 37.8 us -> 0.34 us
  local copies, waits for them, and re-layouts: 77.8 us -> 44.7 us
  matrix products: 9.62 us -> 39.8 us
  blocking collectives: 21.5 us -> 43.5 us
    all_to_all x4 -> x0, waiting for transfers between devices: 178 us -> none  [the longest x1 86.4 us: per_device(): lax.all_to_all(built, 'tok', split_axis=1, concat_axis=1, tiled=True)]
    reduce_scatter x0 -> x1, waiting for transfers between devices: none -> 135 us  [per_device(): lax.psum_scatter(partial, ('tok', 'lyr'), scatter_dimension=0, tiled=True)]
    all_gather x0 -> x2, waiting for transfers between devices: none -> 110 us  [the longest x1 80.2 us: per_device(): gradients = lax.all_gather(gradient, ('tok', 'lyr'), axis=0, tiled=True)]
    psum x1 -> x0, waiting for transfers between devices: 60.2 us -> none  [per_device(): rebuilt = lax.psum(partial_value, 'lyr')]
    unnamed x1 -> x5, waiting for transfers between devices: 0.02 us -> 43.6 us
    all_gather x0 -> x2, blocking collectives: none -> 43.5 us  [the longest x1 23.7 us: per_device(): all_ids = lax.all_gather(block_ids, 'tok', axis=1, tiled=True)]
    all_to_all x4 -> x0, starting transfers between devices: 37.6 us -> none  [the longest x1 21.7 us: per_device(): lax.all_to_all(slot_requests, 'tok', split_axis=1, concat_axis=1, tiled=T...]
    gather x7 -> x0, local copies, waits for them, and re-layouts: 35.4 us -> none  [the longest x4 22.2 us: take_rows(): return jnp.take(table, index, axis=0)]
  transfers between devices with their start and end apart: 5 -> 4, of which waited for: 5 -> 4; matrix products, arithmetic and copies ran while one was open for 4% -> 2% of each run, Pallas kernels for 0% -> 0%
where the time goes in v1:
time: 449 us; the launch traced here: 448 us
  waiting for transfers between devices  289 us (64%)
  local copies, waits for them, and re-layouts  44.7 us (10%)
  blocking collectives  43.5 us (10%)
  matrix products  39.8 us (9%)
  other arithmetic  17.3 us (4%)
  between operations  13.8 us (3%)
    reduce_scatter x1, waiting for transfers between devices, per_device(): lax.psum_scatter(partial, ('tok', 'lyr'), scatter_dimension=0, tiled=True)  135 us
    all_gather x1, waiting for transfers between devices, per_device(): gradients = lax.all_gather(gradient, ('tok', 'lyr'), axis=0, tiled=True)  80.2 us
    unnamed x5, waiting for transfers between devices  43.6 us
    all_gather x1, waiting for transfers between devices, per_device(): all_codes = lax.all_gather(masked, 'tok', axis=1, tiled=True)  30.1 us
    unnamed x8, local copies, waits for them, and re-layouts  28.8 us
    all_gather x1, blocking collectives, per_device(): all_ids = lax.all_gather(block_ids, 'tok', axis=1, tiled=True)  23.7 us
    all_gather x1, blocking collectives, per_device(): all_requests = lax.all_gather(request_ids, 'tok', axis=0, tiled=True)  19.8 us
    dot_general x1, matrix products, per_device(): lax.dot_general(gradients, weights, (((1,), (1,)), ((), ())), preferred_e...  17.2 us
  transfers between devices with their start and end apart: 4, of which 4 were waited for; matrix products, arithmetic and copies ran while one was open for 2% of the time, Pallas kernels for 0%

profile of v1, /device:TPU:0, one launch (start us, length us, event | category | flops | bytes accessed | tf_op | source)
XLA Modules:
  0.0 448.1 jit_solution(1357240671600158753)
XLA Ops:
  7.2 0.0 all-gather.4.cloned.1.call-start
  7.2 0.7 broadcast_compare_fusion
  8.0 2.0 broadcast_select_fusion
  10.0 0.0 all-gather.4.cloned.1.call-update
  10.0 0.0 reduce-scatter.6.cloned.1.call-start
  10.1 23.7 %all_gather.13 = s32[2,2048,2]{1,2,0:T(2,128)S(1)} all-gather(s32[2,128,2]{1,2,0:T(2,128)} %param.7), channel_id=1, replica_groups=mesh['tok'=16,'lyr'=2] {'tok'}, dimensions={1}, use_global_device_ids=true | all-gather | bytes 34816 | tf_op jit(solution)/shard_map/all_gather | solution.py:20
  33.7 0.1 compare_convert_fusion.1
  33.8 30.1 %all-gather.4.cloned.1.call-done = bf16[2,2048,2,256]{3,2,1,0:T(2,128)(2,1)} async-done(((bf16[2,128,2,256]{3,2,1,0:T(2,128)(2,1)}), bf16[2,2048,2,256]{3,2,1,0:T(2,128)(2,1)}) %all-gather.4.cloned.1.call-update) | async-done | bytes 4194320 | tf_op jit(solution)/shard_map/all_gather | solution.py:19
  63.9 2.7 copy.14
  66.6 5.9 %multiply_reduce_fusion.1 = bf16[2,2048,2,256]{3,1,2,0:T(8,128)(2,1)} fusion(bf16[2,2048,2,2]{1,3,2,0:T(2,128)(2,1)S(1)} %compare_convert_fusion.1, bf16[2,2048,2,256]{3,1,2,0:T(8,128)(2,1)S(1)} %copy.14), kind=kLoop, calls=%fused_computation.3 | loop fusion | flops 6291456 | bytes 8421376 | tf_op jit(solution)/shard_map/reduce_sum | solution.py:24
  72.5 6.2 %copy.15 = bf16[2048,2,2,256]{0,3,2,1:T(8,128)(2,1)} copy(bf16[2048,2,2,256]{3,0,2,1:T(8,128)(2,1)} %bitcast.21) | data formatting | bytes 8388608 | tf_op jit(solution)/shard_map/transpose | solution.py:26
  78.7 15.4 %convolution_convert_fusion = bf16[2048,2304]{1,0:T(8,128)(2,1)} fusion(bf16[2048,1024]{0,1:T(8,128)(2,1)} %bitcast.19, bf16[1024,2304]{1,0:T(8,128)(2,1)} %bitcast.29), kind=kOutput, calls=%fused_computation | convolution fusion | flops 9668395008 | bytes 18350080 | tf_op jit(solution)/shard_map/dot_general | solution.py:28
  94.1 0.0 reduce-scatter.6.cloned.1.call-update
  94.2 0.0 all-gather.6.cloned.1.call-start
  94.2 134.8 %reduce-scatter.6.cloned.1.call-done = bf16[64,2304]{1,0:T(8,128)(2,1)} async-done(((bf16[2048,2304]{1,0:T(8,128)(2,1)}), bf16[64,2304]{1,0:T(8,128)(2,1)}) %reduce-scatter.6.cloned.1.call-update) | async-done | bytes 294928 | tf_op jit(solution)/shard_map/reduce_scatter | solution.py:29
  229.0 1.2 multiply_reduce_fusion.2
  230.2 1.8 multiply_convert_fusion
  232.0 0.0 all-gather.6.cloned.1.call-update
  232.0 0.2 reduce-scatter.8.cloned.1.call-start
  232.3 0.1 compare_convert_fusion
  232.4 80.2 %all-gather.6.cloned.1.call-done = bf16[2048,2304]{1,0:T(8,128)(2,1)} async-done(((bf16[64,2304]{1,0:T(8,128)(2,1)}), bf16[2048,2304]{1,0:T(8,128)(2,1)}) %all-gather.6.cloned.1.call-update) | async-done | bytes 9437200 | tf_op jit(solution)/shard_map/all_gather | solution.py:35
  312.6 17.2 %fusion.1 = (bf16[2048,1024]{0,1:T(8,128)(2,1)}, bf16[2048,1024]{0,1:T(8,128)(2,1)}) fusion(bf16[2048,2,2,256]{0,3,2,1:T(8,128)(2,1)} %copy.15, bf16[2048,2304]{1,0:T(8,128)(2,1)} %all-gather.6.cloned.1.call-done, bf16[1024,2304]{1,0:T(8,128)(2,1)} %bitcast.30), kind=kOutput, calls=%fused_computation.5 | convolution fusion | flops 9674162176 | bytes 26738688 | tf_op jit(solution)/shard_map/dot_general | solution.py:36
  329.8 6.2 %copy.16 = bf16[2048,2,2,256]{3,0,2,1:T(8,128)(2,1)} copy(bf16[2048,2,2,256]{0,3,2,1:T(8,128)(2,1)} %bitcast.24) | data formatting | bytes 8388608 | tf_op jit(solution)/shard_map/mul | solution.py:46
  336.0 5.5 %multiply_reduce_fusion = bf16[2048,2,2,256]{3,0,2,1:T(8,128)(2,1)S(1)} fusion(bf16[2048,2,2,2]{0,3,2,1:T(2,128)(2,1)S(1)} %compare_convert_fusion, bf16[2048,2,2,256]{3,0,2,1:T(8,128)(2,1)} %copy.16), kind=kLoop, calls=%fused_computation.1 | loop fusion | flops 6291456 | bytes 8421376 | tf_op jit(solution)/shard_map/reduce_sum | solution.py:45
  341.5 19.1 %copy.22 = bf16[2,2048,2,256]{3,2,0,1:T(2,128)(2,1)} copy(bf16[2,2048,2,256]{3,1,2,0:T(8,128)(2,1)S(1)} %bitcast.22) | data formatting | bytes 8388608
  360.6 7.7 %reshape.71 = bf16[2048,1024]{1,0:T(8,128)(2,1)} reshape(bf16[2048,2,2,256]{3,2,1,0:T(2,128)(2,1)} %bitcast.23) | data formatting | bytes 8388608
  368.4 19.8 %all-gather = s32[16,1,128]{2,1,0:T(1,128)S(1)} all-gather(s32[1,1,128]{2,1,0:T(1,128)S(1)} %bitcast.28), channel_id=1, replica_groups=mesh['tok'=16,'lyr'=2] {'tok'}, dimensions={0}, use_global_device_ids=true | all-gather | bytes 8704 | tf_op jit(solution)/shard_map/all_gather | solution.py:21
  388.2 7.2 %fusion = f32[16,1024]{1,0:T(8,128)S(1)} fusion(bf16[2048,1024]{0,1:T(8,128)(2,1)} %get-tuple-element.3, bf16[2048,1024]{0,1:T(8,128)(2,1)} %bitcast.20, s32[2048]{0:T(1024)S(1)} %bitcast.27), kind=kOutput, calls=%fused_computation.4 | convolution fusion | flops 409010176 | bytes 8462336 | tf_op jit(solution)/shard_map/dot_general | solution.py:41
  395.3 0.7 reshape.68
  396.0 43.5 %reduce-scatter.8.cloned.1.call-done = bf16[128,1024]{1,0:T(8,128)(2,1)} async-done(((bf16[2048,1024]{1,0:T(8,128)(2,1)}), bf16[128,1024]{1,0:T(8,128)(2,1)}) %reduce-scatter.8.cloned.1.call-update) | async-done | bytes 262160
  439.5 1.1 reshape.72
  440.6 0.9 copy.19
  (8 shorter events, 0.0 us)
Async XLA Ops:
  7.2 56.7 %all-gather.4.cloned.1.call-start = ((), (), s32[]{:S(2)}) async-start(), calls=%async_computation.2 | async-start | bytes 4456448 | tf_op jit(solution)/shard_map/all_gather | solution.py:19
  10.0 219.0 %reduce-scatter.6.cloned.1.call-start = ((), (), s32[]{:S(2)}) async-start(), calls=%async_computation.3 | async-start | bytes 9732096 | tf_op jit(solution)/shard_map/reduce_scatter | solution.py:29
  94.1 134.9 %copy-start = (bf16[128,2304]{1,0:T(8,128)(2,1)S(1)}, bf16[128,2304]{1,0:T(8,128)(2,1)}, u32[]{:S(2)}) copy-start(bf16[128,2304]{1,0:T(8,128)(2,1)} %param.10) | copy-start | bytes 1769476
  94.2 218.4 %all-gather.6.cloned.1.call-start = ((), (), s32[]{:S(2)}) async-start(), calls=%async_computation.4 | async-start | bytes 9732096 | tf_op jit(solution)/shard_map/all_gather | solution.py:35
  232.0 207.5 %reduce-scatter.8.cloned.1.call-start = ((), (), s32[]{:S(2)}) async-start(), calls=%async_computation.5 | async-start | bytes 4456448
  360.6 7.7 %copy-start.1 = (s32[128]{0:T(128)S(1)}, s32[128]{0:T(128)}, u32[]{:S(2)}) copy-start(s32[128]{0:T(128)} %param.9) | copy-start | bytes 1540
Sparse Core Ops, SparseCore 0:
  10.7 53.1 all-gather.3
  94.3 134.7 reduce-scatter.5
  232.1 80.4 all-gather.5
  368.5 70.9 reduce-scatter.7

commit v2 on v1

v2 whole, which is shorter than its diff:
```python
import functools

import jax
import jax.numpy as jnp
from jax import lax
from jax.experimental import pallas as pl
from jax.experimental.pallas import tpu as pltpu
from jax.sharding import PartitionSpec as P

REQUESTS = 16
MESH = pl.DeviceIdType.MESH


class Place:
    def __init__(self):
        tok, y = lax.axis_index("tok"), lax.axis_index("lyr")
        z, x, c = tok // 4, (tok // 2) % 2, tok % 2
        self.z, self.c = z, c
        self.inner = (z % 3) != 0
        self.first = (1 - c) * y + c * x
        self.second = (1 - c) * x + c * y
        across_x, across_y = (tok + 2 - 4 * x, y), (tok, 1 - y)
        self.to_first = tuple((1 - c) * a + c * b for a, b in zip(across_y, across_x))
        self.to_second = tuple((1 - c) * a + c * b for a, b in zip(across_x, across_y))
        self.to_core = (tok + 1 - 2 * c, y)
        self.tok, self.y = tok, y
        half = z // 2
        self.near = [z, z + 1 - 2 * (z % 2), 2 - half, 3 - 3 * half]

    def along(self, step):
        return (self.tok + 4 * step, self.y)

    def quarter(self, first, second):
        return (1 - self.c) * (second * 2 + first) + self.c * (first * 2 + second)

    def barrier(self):
        gate = pltpu.get_barrier_semaphore()
        for target in (self.to_first, self.to_second, self.to_core):
            pl.semaphore_signal(gate, inc=1, device_id=target, device_id_type=MESH)

        @pl.when(self.z > 0)
        def _():
            pl.semaphore_signal(gate, inc=1, device_id=self.along(-1), device_id_type=MESH)

        @pl.when(self.z < 3)
        def _():
            pl.semaphore_signal(gate, inc=1, device_id=self.along(1), device_id_type=MESH)

        pl.semaphore_wait(gate, 4 + (self.z % 3 + 1) // 2)


def remote(src, dst, send, recv, target):
    return pltpu.make_async_remote_copy(
        src_ref=src, dst_ref=dst, send_sem=send, recv_sem=recv, device_id=target, device_id_type=MESH
    )


def gather_kernel(own_ref, out_ref, local_sem, recv_sem, core_sem, first_sem, second_sem, z_sem):
    at = Place()
    at.barrier()

    def block(z, first, second, core):
        return (z * 2 + core) * 4 + at.quarter(first, second)

    def mine(j, flip_first, flip_second):
        f = 1 - at.first if flip_first else at.first
        s = 1 - at.second if flip_second else at.second
        return block(at.near[j], f, s, at.c)

    def send(b, sem, target):
        remote(out_ref.at[b], out_ref.at[b], sem, recv_sem.at[b], target).start()

    def arrived(b):
        remote(out_ref.at[b], out_ref.at[b], core_sem.at[0], recv_sem.at[b], at.to_core).wait_recv()

    b0 = mine(0, False, False)
    keep = pltpu.make_async_copy(own_ref, out_ref.at[b0], local_sem)
    keep.start()
    keep.wait()
    used = [0, 0, 0]

    def fan(b, second, first):
        if second:
            send(b, second_sem.at[used[1]], at.to_second)
            used[1] += 1
        if first:
            send(b, first_sem.at[used[0]], at.to_first)
            used[0] += 1
        send(b, core_sem.at[used[2]], at.to_core)
        used[2] += 1

    @pl.when(at.z > 0)
    def _():
        send(b0, z_sem.at[0], at.along(-1))

    @pl.when(at.z < 3)
    def _():
        send(b0, z_sem.at[1], at.along(1))

    fan(b0, True, True)

    def from_z(j):
        b = mine(j, False, False)
        arrived(b)
        step = (3 - 2 * at.z) if j == 1 else (2 * at.z - 3)

        @pl.when(at.inner)
        def _():
            send(b, z_sem.at[1 + j], at.along(step))

        fan(b, True, True)

    def from_second(j):
        b = mine(j, False, True)
        arrived(b)
        fan(b, False, True)

    def from_first(j, flip):
        b = mine(j, True, flip)
        arrived(b)
        fan(b, False, False)

    from_second(0)
    from_z(1)
    from_first(0, False)
    from_second(1)
    from_z(2)
    from_first(0, True)
    from_first(1, False)
    from_second(2)
    from_z(3)
    from_first(1, True)
    from_first(2, False)
    from_second(3)
    from_first(2, True)
    from_first(3, False)
    from_first(3, True)
    for z in range(4):
        for q in range(4):
            arrived((z * 2 + 1 - at.c) * 4 + q)
    for i in range(16):
        remote(own_ref, own_ref, core_sem.at[i], recv_sem.at[0], at.to_core).wait_send()
    for i in range(8):
        remote(own_ref, own_ref, first_sem.at[i], recv_sem.at[0], at.to_core).wait_send()
    for i in range(4):
        remote(own_ref, own_ref, second_sem.at[i], recv_sem.at[0], at.to_core).wait_send()

    @pl.when(at.z > 0)
    def _():
        remote(own_ref, own_ref, z_sem.at[0], recv_sem.at[0], at.to_core).wait_send()

    @pl.when(at.z < 3)
    def _():
        remote(own_ref, own_ref, z_sem.at[1], recv_sem.at[0], at.to_core).wait_send()

    @pl.when(at.inner)
    def _():
        for i in range(2, 5):
            remote(own_ref, own_ref, z_sem.at[i], recv_sem.at[0], at.to_core).wait_send()


def gather_rows(own):
    rows, width = own.shape
    dma = pltpu.SemaphoreType.DMA
    out = pl.pallas_call(
        gather_kernel,
        out_shape=jax.ShapeDtypeStruct((32, rows, width), own.dtype),
        in_specs=[pl.BlockSpec(memory_space=pltpu.VMEM)],
        out_specs=pl.BlockSpec(memory_space=pltpu.VMEM),
        scratch_shapes=[dma, dma((32,)), dma((16,)), dma((8,)), dma((4,)), dma((5,))],
        compiler_params=pltpu.CompilerParams(collective_id=1, has_side_effects=True),
        name="gather_rows",
    )(own)
    return out


def reduce_kernel(
    codes_ref, weights_ref, resid_ref, out_ref,
    held, core_out, core_in, first_out, first_in, second_out, second_in, z_out, z_in,
    core_send, core_recv, first_send, first_recv, second_send, second_recv, z_send, z_recv,
):
    at = Place()
    at.barrier()
    rows, width = out_ref.shape
    depth = codes_ref.shape[-1]
    tile = 256 if width % 256 == 0 else width
    far = at.near[::-1]

    def product(i):
        for core in (1 - at.c, at.c):
            left = codes_ref[far[i] * 2 + core].reshape(4 * rows, depth)
            away = core is not at.c

            @pl.loop(0, width // tile)
            def _(n):
                cols = pl.ds(pl.multiple_of(n * tile, tile), tile)
                value = jnp.dot(left, weights_ref[:, cols], preferred_element_type=jnp.float32)
                value = value.reshape(4, rows, tile)
                if away:
                    core_out[i, :, :, cols] = value.astype(core_out.dtype)
                else:
                    held[i, :, :, cols] = value

            if away:
                core_copy(i).start()

    def core_copy(i):
        return remote(core_out.at[i], core_in.at[i], core_send.at[i], core_recv.at[i], at.to_core)

    def first_copy(i, k):
        return remote(first_out.at[i, k], first_in.at[i, k], first_send.at[i, k], first_recv.at[i, k], at.to_first)

    def second_copy(i):
        return remote(second_out.at[i], second_in.at[i], second_send.at[i], second_recv.at[i], at.to_second)

    def z_copy(i, way, step):
        slot = way * 4 + far[i]
        return remote(z_out.at[i], z_in.at[slot], z_send.at[i], z_recv.at[slot], at.along(step))

    def f32(v):
        return v.astype(jnp.float32)

    def both(i, q):
        return held[i, q] + f32(core_in[i, q])

    def spot(k):
        return 1 - at.second if k == 0 else at.second

    def over_first(i):
        core_copy(i).wait_recv()
        for k in (0, 1):
            first_out[i, k] = both(i, at.quarter(1 - at.first, spot(k))).astype(first_out.dtype)
            first_copy(i, k).start()

    def over_second(i):
        first_copy(i, 0).wait_recv()
        total = both(i, at.quarter(at.first, spot(0))) + f32(first_in[i, 0])
        second_out[i] = total.astype(second_out.dtype)
        second_copy(i).start()

    def z_arrived(slot):
        remote(z_in.at[slot], z_in.at[slot], z_send.at[0], z_recv.at[slot], at.to_core).wait_recv()

    def along_z(i):
        first_copy(i, 1).wait_recv()
        second_copy(i).wait_recv()
        q = at.quarter(at.first, at.second)
        total = both(i, q) + f32(first_in[i, 1]) + f32(second_in[i])
        held[i, q] = total
        if i < 3:
            way = (at.z // 2) if i < 2 else (at.z % 2)
            slot = way * 4 + far[i]

            @pl.when(at.inner)
            def _():
                z_arrived(slot)
                z_out[i] = (held[i, q] + f32(z_in[slot])).astype(z_out.dtype)

            @pl.when(jnp.logical_not(at.inner))
            def _():
                z_out[i] = held[i, q].astype(z_out.dtype)

            z_copy(i, way, 1 - 2 * way).start()
        else:
            @pl.when(at.z > 0)
            def _():
                z_arrived(at.z)
                held[i, q] += f32(z_in[at.z])

            @pl.when(at.z < 3)
            def _():
                z_arrived(4 + at.z)
                held[i, q] += f32(z_in[4 + at.z])

            error = f32(resid_ref[...]) - held[i, q]
            spread = jnp.mean(error * error, axis=-1, keepdims=True)
            out_ref[...] = (error * lax.rsqrt(spread + 1e-06)).astype(out_ref.dtype)

    product(0)
    product(1)
    over_first(0)
    product(2)
    over_first(1)
    over_second(0)
    product(3)
    over_first(2)
    over_second(1)
    along_z(0)
    over_first(3)
    over_second(2)
    along_z(1)
    over_second(3)
    along_z(2)
    along_z(3)
    for i in range(4):
        core_copy(i).wait_send()
        first_copy(i, 0).wait_send()
        first_copy(i, 1).wait_send()
        second_copy(i).wait_send()
        if i < 3:
            remote(z_out.at[i], z_out.at[i], z_send.at[i], z_recv.at[0], at.to_core).wait_send()


def reduce_rows(codes, weights, resid):
    rows, width = resid.shape
    depth = codes.shape[-1]
    dma, bf16 = pltpu.SemaphoreType.DMA, jnp.bfloat16
    vmem = pl.BlockSpec(memory_space=pltpu.VMEM)
    block = (rows, width)
    return pl.pallas_call(
        reduce_kernel,
        out_shape=jax.ShapeDtypeStruct(block, bf16),
        in_specs=[vmem] * 3,
        out_specs=vmem,
        scratch_shapes=[
            pltpu.VMEM((4, 4) + block, jnp.float32),
            pltpu.VMEM((4, 4) + block, bf16),
            pltpu.VMEM((4, 4) + block, bf16),
            pltpu.VMEM((4, 2) + block, bf16),
            pltpu.VMEM((4, 2) + block, bf16),
            pltpu.VMEM((4,) + block, bf16),
            pltpu.VMEM((4,) + block, bf16),
            pltpu.VMEM((3,) + block, bf16),
            pltpu.VMEM((8,) + block, bf16),
            dma((4,)), dma((4,)), dma((4, 2)), dma((4, 2)), dma((4,)), dma((4,)), dma((3,)), dma((8,)),
        ],
        compiler_params=pltpu.CompilerParams(
            collective_id=2, has_side_effects=True, vmem_limit_bytes=60 * 1024 * 1024
        ),
        name="reduce_rows",
    )(codes, weights, resid)


def blocked(table, rows):
    rest = table.shape[1:]
    return jnp.swapaxes(table.reshape((4, 2, 2, 2, rows) + rest), 1, 2).reshape((8, 4, rows) + rest)


def unblocked(table):
    rows, rest = table.shape[1], table.shape[2:]
    return jnp.swapaxes(table.reshape((4, 2, 2, 2, rows) + rest), 1, 2).reshape((32 * rows,) + rest)


def per_device(feature_codes, block_ids, target_layer, request_ids, target_resid, decoder, grid=False):
    layers_here, count, kact, panel = feature_codes.shape
    width = target_resid.shape[1]
    features = decoder.shape[1]
    per_dev = features // panel
    tok, lyr = lax.axis_index("tok"), lax.axis_index("lyr")
    lyr_count = lax.axis_size("lyr")
    layer_ids = lyr * layers_here + jnp.arange(layers_here, dtype=jnp.int32)
    alive = layer_ids[:, None] <= target_layer[None, :]
    masked = jnp.where(alive[:, :, None, None], feature_codes, jnp.zeros_like(feature_codes))
    all_codes = lax.all_gather(masked, "tok", axis=1, tiled=True)
    numbers = jnp.concatenate(
        [jnp.moveaxis(block_ids, 1, 2).reshape(layers_here * kact, count), request_ids[None, :]], axis=0
    )
    numbers = lax.all_gather(numbers, "tok", axis=1, tiled=True)
    all_ids = jnp.moveaxis(numbers[:-1].reshape(layers_here, kact, -1), 1, 2)
    all_requests = numbers[-1]
    mine = tok * per_dev + jnp.arange(per_dev, dtype=jnp.int32)
    named = (all_ids[..., None] == mine).astype(jnp.bfloat16)
    dense = jnp.sum(all_codes[:, :, :, None, :] * named[..., None], axis=2)
    tokens = dense.shape[1]
    dense = jnp.swapaxes(dense, 0, 1).reshape(tokens, layers_here * features)
    weights = decoder.reshape(layers_here * features, width)
    rows = count // lyr_count
    resid = lax.dynamic_slice_in_dim(target_resid, lyr * rows, rows, 0)
    if grid:
        gradient = reduce_rows(blocked(dense, rows), weights, resid)
        gradients = unblocked(gather_rows(gradient))
    else:
        partial = jnp.dot(dense, weights, preferred_element_type=jnp.float32).astype(jnp.bfloat16)
        rebuilt = lax.psum_scatter(partial, ("tok", "lyr"), scatter_dimension=0, tiled=True)
        error = resid.astype(jnp.float32) - rebuilt.astype(jnp.float32)
        spread = jnp.mean(error * error, axis=-1, keepdims=True)
        gradient = (error * lax.rsqrt(spread + 1e-06)).astype(jnp.bfloat16)
        gradients = lax.all_gather(gradient, ("tok", "lyr"), axis=0, tiled=True)
    projected = lax.dot_general(
        gradients, weights, (((1,), (1,)), ((), ())), preferred_element_type=jnp.float32
    ).astype(jnp.bfloat16)
    attribution = dense.astype(jnp.float32) * projected.astype(jnp.float32)
    members = (all_requests[:, None] == jnp.arange(REQUESTS, dtype=jnp.int32)).astype(jnp.float32)
    totals = lax.dot_general(
        members, attribution, (((0,), (0,)), ((), ())), precision=lax.Precision.HIGHEST
    ).reshape(REQUESTS, layers_here, features)
    scored = attribution.astype(jnp.bfloat16).reshape(tokens, layers_here, 1, per_dev, panel)
    spread_out = jnp.sum(
        scored * jnp.swapaxes(named, 0, 1)[..., None], axis=3
    )
    scores = lax.psum_scatter(
        jnp.swapaxes(spread_out, 0, 1), "tok", scatter_dimension=1, tiled=True
    )
    return (scores, totals)


def solution(mesh):
    placed = (
        P("lyr", "tok", None, None),
        P("lyr", "tok", None),
        P("tok"),
        P("tok"),
        P("tok", None),
        P("lyr", "tok", None),
    )
    wide = len({getattr(d, "coords", (0,))[0] for d in mesh.devices.flat})
    grid = (mesh.shape["tok"], mesh.shape["lyr"]) == (16, 2) and wide == 2
    return jax.shard_map(
        functools.partial(per_device, grid=grid),
        mesh=mesh,
        in_specs=placed,
        out_specs=(P("lyr", "tok", None, None), P(None, "lyr", "tok")),
        check_vma=False,
    )
```

time: 449 us -> 375 us (0.84)
  waiting for transfers between devices: 289 us -> 94.7 us
  Pallas kernels: 0 us -> 112 us
  local copies, waits for them, and re-layouts: 44.7 us -> 87.9 us
  blocking collectives: 43.5 us -> 23.4 us
  matrix products: 39.8 us -> 24.8 us
    reduce_scatter x1 -> x0, waiting for transfers between devices: 135 us -> none  [per_device(): lax.psum_scatter(partial, ('tok', 'lyr'), scatter_dimension=0, tiled=True)]
    pallas_call x0 -> x2, Pallas kernels: none -> 112 us  [the longest x1 59.1 us: reduce_rows(): pl.pallas_call(reduce_kernel, out_shape=jax.ShapeDtypeStruct(block, bf16)...]
    all_gather x1 -> x0, waiting for transfers between devices: 80.2 us -> none  [per_device(): gradients = lax.all_gather(gradient, ('tok', 'lyr'), axis=0, tiled=True)]
    unnamed x5 -> x3, waiting for transfers between devices: 43.6 us -> 65.9 us
    all_gather x2 -> x1, blocking collectives: 43.5 us -> 23.4 us  [per_device(): numbers = lax.all_gather(numbers, 'tok', axis=1, tiled=True)]
    dot_general x1 -> x0, matrix products: 15.4 us -> none  [per_device(): jnp.dot(dense, weights, preferred_element_type=jnp.float32)]
    transpose x1, local copies, waits for them, and re-layouts: 6.23 us -> 19 us  [per_device(): dense = jnp.swapaxes(dense, 0, 1).reshape(tokens, layers_here * features)]
    convert_element_type x0 -> x1, local copies, waits for them, and re-layouts: none -> 8.7 us  [per_device(): attribution = dense.astype(jnp.float32) * projected.astype(jnp.float32)]
  transfers between devices with their start and end apart: 4 -> 2, of which waited for: 4 -> 2; matrix products, arithmetic and copies ran while one was open for 2% -> 2% of each run, Pallas kernels for 0% -> 0%
where the time goes in v2:
time: 375 us; the launch traced here: 374 us
  Pallas kernels  112 us (30%)
  waiting for transfers between devices  94.7 us (25%)
  local copies, waits for them, and re-layouts  87.9 us (23%)
  matrix products  24.8 us (7%)
  blocking collectives  23.4 us (6%)
  other arithmetic  17.1 us (5%)
  between operations  14.1 us (4%)
    unnamed x3, waiting for transfers between devices  65.9 us
    pallas_call x1, Pallas kernels, reduce_rows(): pl.pallas_call(reduce_kernel, out_shape=jax.ShapeDtypeStruct(block, bf16)...  59.1 us
    pallas_call x1, Pallas kernels, gather_rows(): pl.pallas_call(gather_kernel, out_shape=jax.ShapeDtypeStruct((32, rows, w...  52.6 us
    unnamed x8, local copies, waits for them, and re-layouts  28.9 us
    all_gather x1, waiting for transfers between devices, per_device(): all_codes = lax.all_gather(masked, 'tok', axis=1, tiled=True)  28.8 us
    all_gather x1, blocking collectives, per_device(): numbers = lax.all_gather(numbers, 'tok', axis=1, tiled=True)  23.4 us
    transpose x1, local copies, waits for them, and re-layouts, per_device(): dense = jnp.swapaxes(dense, 0, 1).reshape(tokens, layers_here * features)  19 us
    dot_general x1, matrix products, per_device(): lax.dot_general(gradients, weights, (((1,), (1,)), ((), ())), preferred_e...  18.5 us
  transfers between devices with their start and end apart: 2, of which 2 were waited for; matrix products, arithmetic and copies ran while one was open for 2% of the time, Pallas kernels for 0%

profile of v2, /device:TPU:0, one launch (start us, length us, event | category | flops | bytes accessed | tf_op | source)
XLA Modules:
  0.0 373.9 jit_solution(9921165932095676583)
XLA Ops:
  7.2 0.0 all-gather.2.cloned.1.call-start
  7.2 0.8 broadcast_compare_fusion
  8.0 2.0 broadcast_select_fusion
  10.1 0.0 all-gather.2.cloned.1.call-update
  10.1 0.0 reduce-scatter.5.cloned.1.call-start
  10.1 0.7 pad_add_fusion
  10.8 23.4 %all_gather.7 = s32[5,2048]{1,0:T(8,128)S(1)} all-gather(s32[5,128]{1,0:T(8,128)S(1)} %pad_add_fusion), channel_id=1, replica_groups=mesh['tok'=16,'lyr'=2] {'tok'}, dimensions={1}, use_global_device_ids=true | all-gather | bytes 43520 | tf_op jit(solution)/shard_map/all_gather | solution.py:358
  34.3 0.7 constant_dynamic-slice_fusion.resid_ref
  35.0 0.1 compare_convert_fusion.1
  35.1 0.1 compare_convert_fusion
  35.2 28.8 %all-gather.2.cloned.1.call-done = bf16[2,2048,2,256]{3,2,1,0:T(2,128)(2,1)} async-done(((bf16[2,128,2,256]{3,2,1,0:T(2,128)(2,1)}), bf16[2,2048,2,256]{3,2,1,0:T(2,128)(2,1)}) %all-gather.2.cloned.1.call-update) | async-done | bytes 4194320 | tf_op jit(solution)/shard_map/all_gather | solution.py:354
  64.0 2.7 copy.23
  66.7 3.9 %multiply_reduce_fusion.1 = bf16[2,2048,2,256]{3,1,2,0:T(8,128)(2,1)S(1)} fusion(bf16[2,2048,2,2]{1,3,2,0:T(2,128)(2,1)S(1)} %compare_convert_fusion.1, bf16[2,2048,2,256]{3,1,2,0:T(8,128)(2,1)S(1)} %copy.23), kind=kLoop, calls=%fused_computation.2 | loop fusion | flops 6291456 | bytes 8421376 | tf_op jit(solution)/shard_map/reduce_sum | solution.py:363
  70.7 4.0 %bitcast_convert_fusion = f32[2048,2,2,256]{3,0,2,1:T(8,128)} fusion(bf16[2,2048,2,256]{3,1,2,0:T(8,128)(2,1)S(1)} %multiply_reduce_fusion.1), kind=kLoop, calls=%fused_computation.16 | loop fusion | flops 2097152 | bytes 12582912 | tf_op jit(solution)/shard_map/convert_element_type | solution.py:382
  74.6 19.0 %copy.25 = bf16[2048,2,2,256]{3,2,1,0:T(2,128)(2,1)} copy(bf16[2048,2,2,256]{3,0,2,1:T(8,128)(2,1)S(1)} %bitcast.29) | data formatting | bytes 8388608 | tf_op jit(solution)/shard_map/transpose | solution.py:365
  93.6 7.8 %reshape_reshape.3 = bf16[4,2,2,2,64,1024]{5,4,3,2,1,0:T(8,128)(2,1)} reshape(bf16[2048,2,2,256]{3,2,1,0:T(2,128)(2,1)} %copy.25) | data formatting | bytes 8388608 | tf_op jit(solution)/shard_map/reshape;reshape | solution.py:336
  101.4 4.9 %copy.26 = bf16[4,2,2,2,64,1024]{5,4,3,2,1,0:T(8,128)(2,1)} copy(bf16[4,2,2,2,64,1024]{5,4,3,1,2,0:T(8,128)(2,1)} %bitcast.33) | data formatting | bytes 8388608 | tf_op jit(solution)/shard_map/transpose | solution.py:336
  106.2 8.7 %copy.24 = f32[2048,2,2,256]{0,3,2,1:T(8,128)} copy(f32[2048,2,2,256]{3,0,2,1:T(8,128)} %bitcast_convert_fusion) | data formatting | bytes 16777216 | tf_op jit(solution)/shard_map/convert_element_type | solution.py:382
  115.0 59.1 %reduce_rows.1.own_ref = bf16[64,2304]{1,0:T(8,128)(2,1)} custom-call(bf16[8,4,64,1024]{3,2,1,0:T(8,128)(2,1)} %bitcast.31, bf16[1024,2304]{1,0:T(8,128)(2,1)} %bitcast.36, bf16[64,2304]{1,0:T(8,128)(2,1)} %constant_dynamic-slice_fusion.resid_ref), custom_call_target="tpu_custom_call" | custom-call | tf_op jit(solution)/shard_map/reduce_rows/pallas_call | solution.py:310
  174.0 52.6 %gather_rows.1 = bf16[32,64,2304]{2,1,0:T(8,128)(2,1)} custom-call(bf16[64,2304]{1,0:T(8,128)(2,1)} %reduce_rows.1.own_ref), custom_call_target="tpu_custom_call" | custom-call | tf_op jit(solution)/shard_map/gather_rows/pallas_call | solution.py:165
  226.7 8.3 %copy.27 = bf16[4,2,2,2,64,2304]{5,4,3,1,2,0:T(8,128)(2,1)} copy(bf16[4,2,2,2,64,2304]{5,4,3,2,1,0:T(8,128)(2,1)} %bitcast.30) | data formatting | bytes 18874368 | tf_op jit(solution)/shard_map/reshape | solution.py:341
  235.0 18.5 %fusion.4 = (bf16[2048,1024]{0,1:T(8,128)(2,1)}, f32[2048,1024]{0,1:T(8,128)}) fusion(bf16[2048,2304]{1,0:T(8,128)(2,1)} %bitcast.35, bf16[1024,2304]{1,0:T(8,128)(2,1)} %bitcast.37, f32[2048,2,2,256]{0,3,2,1:T(8,128)} %copy.24), kind=kOutput, calls=%fused_computation.17 | convolution fusion | flops 9672065024 | bytes 35127296 | tf_op jit(solution)/shard_map/dot_general | solution.py:379
  253.4 6.2 %copy.28 = bf16[2048,2,2,256]{3,0,2,1:T(8,128)(2,1)} copy(bf16[2048,2,2,256]{0,3,2,1:T(8,128)(2,1)} %bitcast.38) | data formatting | bytes 8388608 | tf_op jit(solution)/shard_map/mul | solution.py:389
  259.6 5.5 %multiply_reduce_fusion = bf16[2048,2,2,256]{3,0,2,1:T(8,128)(2,1)S(1)} fusion(bf16[2048,2,2,2]{0,3,2,1:T(2,128)(2,1)S(1)} %compare_convert_fusion, bf16[2048,2,2,256]{3,0,2,1:T(8,128)(2,1)} %copy.28), kind=kLoop, calls=%fused_computation.1 | loop fusion | flops 6291456 | bytes 8421376 | tf_op jit(solution)/shard_map/reduce_sum | solution.py:388
  265.2 19.1 %copy.34 = bf16[2,2048,2,256]{3,2,0,1:T(2,128)(2,1)} copy(bf16[2,2048,2,256]{3,1,2,0:T(8,128)(2,1)S(1)} %bitcast.32) | data formatting | bytes 8388608
  284.2 7.8 %reshape.82 = bf16[2048,1024]{1,0:T(8,128)(2,1)} reshape(bf16[2048,2,2,256]{3,2,1,0:T(2,128)(2,1)} %bitcast.34) | data formatting | bytes 8388608
  292.0 0.0 reduce-scatter.5.cloned.1.call-update
  292.0 6.4 %fusion.1 = f32[16,1024]{1,0:T(8,128)S(1)} fusion(f32[2048,1024]{0,1:T(8,128)} %get-tuple-element.3, s32[2048]{0:T(1024)S(1)} %bitcast.42), kind=kOutput, calls=%fused_computation.6 | convolution fusion | flops 402718720 | bytes 8462336 | tf_op jit(solution)/shard_map/dot_general | solution.py:384
  298.4 0.7 reshape.80
  299.1 65.9 %reduce-scatter.5.cloned.1.call-done = bf16[128,1024]{1,0:T(8,128)(2,1)} async-done(((bf16[2048,1024]{1,0:T(8,128)(2,1)}), bf16[128,1024]{1,0:T(8,128)(2,1)}) %reduce-scatter.5.cloned.1.call-update) | async-done | bytes 262160
  365.0 1.1 reshape.83
  366.2 0.9 copy.31
  (9 shorter events, 0.1 us)
Async XLA Ops:
  7.2 27.1 %copy-start = (bf16[128,2304]{1,0:T(8,128)(2,1)S(1)}, bf16[128,2304]{1,0:T(8,128)(2,1)}, u32[]{:S(2)}) copy-start(bf16[128,2304]{1,0:T(8,128)(2,1)} %param.10) | copy-start | bytes 1769476
  7.2 56.8 %all-gather.2.cloned.1.call-start = ((), (), s32[]{:S(2)}) async-start(), calls=%async_computation.1 | async-start | bytes 4456448 | tf_op jit(solution)/shard_map/all_gather | solution.py:354
  10.1 355.0 %reduce-scatter.5.cloned.1.call-start = ((), (), s32[]{:S(2)}) async-start(), calls=%async_computation.2 | async-start | bytes 4456448
  284.2 82.8 %copy-start.1 = (bf16[128,2304]{1,0:T(8,128)(2,1)S(1)}, bf16[128,2304]{1,0:T(8,128)(2,1)}, u32[]{:S(2)}) copy-start(bf16[128,2304]{1,0:T(8,128)(2,1)} %param.10) | copy-start | bytes 1769476
Sparse Core Ops, SparseCore 0:
  10.7 53.1 all-gather.1
  292.1 72.8 reduce-scatter.4

commit v3 on v2

--- a/solution.py
+++ b/solution.py
@@ -8,6 +8,7 @@
 from jax.sharding import PartitionSpec as P
 
 REQUESTS = 16
+CAP = 16
 MESH = pl.DeviceIdType.MESH
 
 
@@ -33,20 +34,32 @@
     def quarter(self, first, second):
         return (1 - self.c) * (second * 2 + first) + self.c * (first * 2 + second)
 
+    def peer(self, distance):
+        return ((self.tok + distance) % 16, self.y)
+
     def barrier(self):
         gate = pltpu.get_barrier_semaphore()
-        for target in (self.to_first, self.to_second, self.to_core):
-            pl.semaphore_signal(gate, inc=1, device_id=target, device_id_type=MESH)
-
-        @pl.when(self.z > 0)
-        def _():
-            pl.semaphore_signal(gate, inc=1, device_id=self.along(-1), device_id_type=MESH)
-
-        @pl.when(self.z < 3)
-        def _():
-            pl.semaphore_signal(gate, inc=1, device_id=self.along(1), device_id_type=MESH)
-
-        pl.semaphore_wait(gate, 4 + (self.z % 3 + 1) // 2)
+        for distance in range(1, 16):
+            pl.semaphore_signal(gate, inc=1, device_id=self.peer(distance), device_id_type=MESH)
+        pl.semaphore_signal(gate, inc=1, device_id=(self.tok, 1 - self.y), device_id_type=MESH)
+        pl.semaphore_wait(gate, 16)
+
+
+def earlier(count):
+    shape = (count, count)
+    return (lax.broadcasted_iota(jnp.int32, shape, 0) < lax.broadcasted_iota(jnp.int32, shape, 1)).astype(jnp.bfloat16)
+
+
+def slots(numbers, layer, first_panel, panels):
+    shape = (panels * CAP, numbers.shape[1])
+    row = lax.broadcasted_iota(jnp.int32, shape, 0)
+    panel = row // CAP + first_panel
+    rank = (row % CAP).astype(jnp.float32)
+    named = [numbers[2 * layer + k : 2 * layer + k + 1] == panel for k in (0, 1)]
+    either = jnp.where(named[0] | named[1], 1.0, 0.0).astype(jnp.bfloat16)
+    before = jnp.dot(either, earlier(shape[1]), preferred_element_type=jnp.float32)
+    here = before == rank
+    return [jnp.where(n & here, 1.0, 0.0).astype(jnp.bfloat16) for n in named]
 
 
 def remote(src, dst, send, recv, target):
@@ -55,7 +68,10 @@
     )
 
 
-def gather_kernel(own_ref, out_ref, local_sem, recv_sem, core_sem, first_sem, second_sem, z_sem):
+def gather_kernel(
+    own_ref, dense_ref, weights_ref, numbers_ref, local_numbers_ref, scores_ref, totals_ref,
+    out_ref, slot_out, slot_in, local_sem, recv_sem, core_sem, first_sem, second_sem, z_sem, slot_send, slot_recv,
+):
     at = Place()
     at.barrier()
 
@@ -119,6 +135,56 @@
         b = mine(j, True, flip)
         arrived(b)
         fan(b, False, False)
+
+    rows = out_ref.shape[1]
+    panel = slot_out.shape[-1]
+    totals_ref[...] = jnp.zeros_like(totals_ref)
+
+    def slot_copy(source):
+        return remote(
+            slot_out.at[source], slot_in.at[at.tok], slot_send.at[source], slot_recv.at[at.tok], (source, at.y)
+        )
+
+    def project(z, core, own):
+        group = z * 2 + core
+        left = out_ref[pl.ds(group * 4, 4)].reshape(4 * rows, out_ref.shape[2])
+        sources = [(z * 2 + x) * 2 + core for x in (0, 1)]
+        numbers = [numbers_ref[source] for source in sources]
+        members = []
+        for x in (0, 1):
+            wanted = lax.broadcasted_iota(jnp.int32, (REQUESTS, 2 * rows), 0)
+            members.append(jnp.where(numbers[x][4:5] == wanted, 1.0, 0.0).astype(jnp.bfloat16))
+        for n in range(4):
+            layer, which = n // 2, n % 2
+            cols = slice(n * panel, (n + 1) * panel)
+            product = lax.dot_general(
+                left, weights_ref[cols, :], (((1,), (1,)), ((), ())), preferred_element_type=jnp.float32
+            ).astype(jnp.bfloat16)
+            for x in (0, 1):
+                span = slice(x * 2 * rows, (x + 1) * 2 * rows)
+                value = product[span].astype(jnp.float32) * dense_ref[group, x, :, cols].astype(jnp.float32)
+                high = value.astype(jnp.bfloat16)
+                low = (value - high.astype(jnp.float32)).astype(jnp.bfloat16)
+                totals_ref[:, cols] += jnp.dot(members[x], high, preferred_element_type=jnp.float32) + jnp.dot(
+                    members[x], low, preferred_element_type=jnp.float32
+                )
+                held = slots(numbers[x], layer, at.tok * 2 + which, 1)
+                packed = jnp.dot(held[0] + held[1], high, preferred_element_type=jnp.float32).astype(jnp.bfloat16)
+                slot_out[sources[x], layer, which * CAP : (which + 1) * CAP, :] = packed
+        for x in (0, 1):
+            if own:
+
+                @pl.when(sources[x] != at.tok)
+                def _():
+                    slot_copy(sources[x]).start()
+
+            else:
+                slot_copy(sources[x]).start()
+
+    def from_core(j):
+        for q in range(4):
+            arrived((at.near[j] * 2 + 1 - at.c) * 4 + q)
+        project(at.near[j], 1 - at.c, False)
 
     from_second(0)
     from_z(1)
@@ -130,14 +196,37 @@
     from_second(2)
     from_z(3)
     from_first(1, True)
+    project(at.near[0], at.c, True)
     from_first(2, False)
     from_second(3)
+    from_core(0)
+    project(at.near[1], at.c, False)
     from_first(2, True)
+    project(at.near[2], at.c, False)
     from_first(3, False)
+    from_core(1)
     from_first(3, True)
-    for z in range(4):
-        for q in range(4):
-            arrived((z * 2 + 1 - at.c) * 4 + q)
+    from_core(2)
+    project(at.near[3], at.c, False)
+    from_core(3)
+    slot_in[at.tok] = slot_out[at.tok]
+    for distance in range(1, 16):
+        source = (at.tok + distance) % 16
+        remote(
+            slot_out.at[0], slot_in.at[source], slot_send.at[0], slot_recv.at[source], at.to_core
+        ).wait_recv()
+    for layer in (0, 1):
+        held = slots(local_numbers_ref[...], layer, 0, 32)
+        table = slot_in[:, layer].reshape(32 * CAP, panel)
+        for k in (0, 1):
+            scores_ref[2 * layer + k] = lax.dot_general(
+                held[k], table, (((0,), (0,)), ((), ())), preferred_element_type=jnp.float32
+            ).astype(scores_ref.dtype)
+    for distance in range(1, 16):
+        source = (at.tok + distance) % 16
+        remote(
+            slot_out.at[0], slot_in.at[0], slot_send.at[source], slot_recv.at[0], at.to_core
+        ).wait_send()
     for i in range(16):
         remote(own_ref, own_ref, core_sem.at[i], recv_sem.at[0], at.to_core).wait_send()
     for i in range(8):
@@ -159,30 +248,85 @@
             remote(own_ref, own_ref, z_sem.at[i], recv_sem.at[0], at.to_core).wait_send()
 
 
-def gather_rows(own):
+def gather_rows(own, dense, weights, numbers, local_numbers, panel):
     rows, width = own.shape
-    dma = pltpu.SemaphoreType.DMA
-    out = pl.pallas_call(
+    dma, bf16 = pltpu.SemaphoreType.DMA, jnp.bfloat16
+    vmem = pl.BlockSpec(memory_space=pltpu.VMEM)
+    return pl.pallas_call(
         gather_kernel,
-        out_shape=jax.ShapeDtypeStruct((32, rows, width), own.dtype),
-        in_specs=[pl.BlockSpec(memory_space=pltpu.VMEM)],
-        out_specs=pl.BlockSpec(memory_space=pltpu.VMEM),
-        scratch_shapes=[dma, dma((32,)), dma((16,)), dma((8,)), dma((4,)), dma((5,))],
-        compiler_params=pltpu.CompilerParams(collective_id=1, has_side_effects=True),
+        out_shape=(
+            jax.ShapeDtypeStruct((4, 2 * rows, panel), bf16),
+            jax.ShapeDtypeStruct((REQUESTS, weights.shape[0]), jnp.float32),
+        ),
+        in_specs=[vmem] * 5,
+        out_specs=(vmem, vmem),
+        scratch_shapes=[
+            pltpu.VMEM((32, rows, width), bf16),
+            pltpu.VMEM((16, 2, 2 * CAP, panel), bf16),
+            pltpu.VMEM((16, 2, 2 * CAP, panel), bf16),
+            dma, dma((32,)), dma((16,)), dma((8,)), dma((4,)), dma((5,)), dma((16,)), dma((16,)),
+        ],
+        compiler_params=pltpu.CompilerParams(
+            collective_id=1, has_side_effects=True, vmem_limit_bytes=60 * 1024 * 1024
+        ),
         name="gather_rows",
-    )(own)
-    return out
+    )(own, dense, weights, numbers, local_numbers)
 
 
 def reduce_kernel(
-    codes_ref, weights_ref, resid_ref, out_ref,
-    held, core_out, core_in, first_out, first_in, second_out, second_in, z_out, z_in,
+    masked_ref, local_numbers_ref, weights_ref, resid_ref, out_ref, codes_ref, numbers_ref,
+    packed, slot_in, slot_send, slot_recv, number_send, number_recv, held, core_out, core_in, first_out, first_in, second_out, second_in, z_out, z_in,
     core_send, core_recv, first_send, first_recv, second_send, second_recv, z_send, z_recv,
 ):
     at = Place()
     at.barrier()
     rows, width = out_ref.shape
     depth = codes_ref.shape[-1]
+    panel = packed.shape[-1]
+    local = local_numbers_ref[...]
+    numbers_ref[at.tok] = local
+    for layer in (0, 1):
+        sent = slots(local, layer, 0, 32)
+        value = sum(
+            jnp.dot(sent[k], masked_ref[2 * layer + k], preferred_element_type=jnp.float32) for k in (0, 1)
+        )
+        packed[:, layer] = value.astype(packed.dtype).reshape(16, 2 * CAP, panel)
+
+    def slot_copies(distance):
+        target = (at.tok + distance) % 16
+        return (
+            remote(
+                packed.at[target], slot_in.at[at.tok], slot_send.at[distance], slot_recv.at[distance], (target, at.y)
+            ),
+            remote(
+                local_numbers_ref, numbers_ref.at[at.tok], number_send.at[distance], number_recv.at[distance],
+                (target, at.y),
+            ),
+        )
+
+    for distance in range(1, 16):
+        for copy in slot_copies(distance):
+            copy.start()
+    slot_in[at.tok] = packed[at.tok]
+    for distance in range(1, 16):
+        for copy in slot_copies(distance):
+            copy.wait_recv()
+
+    @pl.loop(0, 16)
+    def _(source):
+        for layer in (0, 1):
+            held_slots = slots(numbers_ref[source], layer, at.tok * 2, 2)
+            hot = held_slots[0] + held_slots[1]
+            for which in (0, 1):
+                part = slice(which * CAP, (which + 1) * CAP)
+                n = 2 * layer + which
+                codes_ref[(source // 4) * 2 + source % 2, (source // 2) % 2, :, n * panel : (n + 1) * panel] = (
+                    lax.dot_general(
+                        hot[part], slot_in[source, layer, part, :], (((0,), (0,)), ((), ())),
+                        preferred_element_type=jnp.float32,
+                    ).astype(codes_ref.dtype)
+                )
+
     tile = 256 if width % 256 == 0 else width
     far = at.near[::-1]
 
@@ -292,6 +436,9 @@
     over_second(3)
     along_z(2)
     along_z(3)
+    for distance in range(1, 16):
+        for copy in slot_copies(distance):
+            copy.wait_send()
     for i in range(4):
         core_copy(i).wait_send()
         first_copy(i, 0).wait_send()
@@ -301,18 +448,26 @@
             remote(z_out.at[i], z_out.at[i], z_send.at[i], z_recv.at[0], at.to_core).wait_send()
 
 
-def reduce_rows(codes, weights, resid):
+def reduce_rows(masked, local_numbers, weights, resid):
     rows, width = resid.shape
-    depth = codes.shape[-1]
+    depth = weights.shape[0]
+    panel = masked.shape[-1]
     dma, bf16 = pltpu.SemaphoreType.DMA, jnp.bfloat16
     vmem = pl.BlockSpec(memory_space=pltpu.VMEM)
     block = (rows, width)
     return pl.pallas_call(
         reduce_kernel,
-        out_shape=jax.ShapeDtypeStruct(block, bf16),
-        in_specs=[vmem] * 3,
-        out_specs=vmem,
+        out_shape=(
+            jax.ShapeDtypeStruct(block, bf16),
+            jax.ShapeDtypeStruct((8, 2, 2 * rows, depth), bf16),
+            jax.ShapeDtypeStruct((16,) + local_numbers.shape, jnp.int32),
+        ),
+        in_specs=[vmem] * 4,
+        out_specs=(vmem,) * 3,
         scratch_shapes=[
+            pltpu.VMEM((16, 2, 2 * CAP, panel), bf16),
+            pltpu.VMEM((16, 2, 2 * CAP, panel), bf16),
+            dma((16,)), dma((16,)), dma((16,)), dma((16,)),
             pltpu.VMEM((4, 4) + block, jnp.float32),
             pltpu.VMEM((4, 4) + block, bf16),
             pltpu.VMEM((4, 4) + block, bf16),
@@ -328,17 +483,7 @@
             collective_id=2, has_side_effects=True, vmem_limit_bytes=60 * 1024 * 1024
         ),
         name="reduce_rows",
-    )(codes, weights, resid)
-
-
-def blocked(table, rows):
-    rest = table.shape[1:]
-    return jnp.swapaxes(table.reshape((4, 2, 2, 2, rows) + rest), 1, 2).reshape((8, 4, rows) + rest)
-
-
-def unblocked(table):
-    rows, rest = table.shape[1], table.shape[2:]
-    return jnp.swapaxes(table.reshape((4, 2, 2, 2, rows) + rest), 1, 2).reshape((32 * rows,) + rest)
+    )(masked, local_numbers, weights, resid)
 
 
 def per_device(feature_codes, block_ids, target_layer, request_ids, target_resid, decoder, grid=False):
@@ -351,10 +496,20 @@
     layer_ids = lyr * layers_here + jnp.arange(layers_here, dtype=jnp.int32)
     alive = layer_ids[:, None] <= target_layer[None, :]
     masked = jnp.where(alive[:, :, None, None], feature_codes, jnp.zeros_like(feature_codes))
-    all_codes = lax.all_gather(masked, "tok", axis=1, tiled=True)
     numbers = jnp.concatenate(
         [jnp.moveaxis(block_ids, 1, 2).reshape(layers_here * kact, count), request_ids[None, :]], axis=0
     )
+    weights = decoder.reshape(layers_here * features, width)
+    rows = count // lyr_count
+    resid = lax.dynamic_slice_in_dim(target_resid, lyr * rows, rows, 0)
+    if grid:
+        numbers = jnp.concatenate([numbers, jnp.zeros((8 - numbers.shape[0], count), jnp.int32)], axis=0)
+        by_k = jnp.moveaxis(masked, 1, 2).reshape(layers_here * kact, count, panel)
+        gradient, dense, all_numbers = reduce_rows(by_k, numbers, weights, resid)
+        scores, totals = gather_rows(gradient, dense, weights, all_numbers, numbers, panel)
+        scores = jnp.moveaxis(scores.reshape(layers_here, kact, count, panel), 1, 2)
+        return (scores, totals.reshape(REQUESTS, layers_here, features))
+    all_codes = lax.all_gather(masked, "tok", axis=1, tiled=True)
     numbers = lax.all_gather(numbers, "tok", axis=1, tiled=True)
     all_ids = jnp.moveaxis(numbers[:-1].reshape(layers_here, kact, -1), 1, 2)
     all_requests = numbers[-1]
@@ -363,19 +518,12 @@
     dense = jnp.sum(all_codes[:, :, :, None, :] * named[..., None], axis=2)
     tokens = dense.shape[1]
     dense = jnp.swapaxes(dense, 0, 1).reshape(tokens, layers_here * features)
-    weights = decoder.reshape(layers_here * features, width)
-    rows = count // lyr_count
-    resid = lax.dynamic_slice_in_dim(target_resid, lyr * rows, rows, 0)
-    if grid:
-        gradient = reduce_rows(blocked(dense, rows), weights, resid)
-        gradients = unblocked(gather_rows(gradient))
-    else:
-        partial = jnp.dot(dense, weights, preferred_element_type=jnp.float32).astype(jnp.bfloat16)
-        rebuilt = lax.psum_scatter(partial, ("tok", "lyr"), scatter_dimension=0, tiled=True)
-        error = resid.astype(jnp.float32) - rebuilt.astype(jnp.float32)
-        spread = jnp.mean(error * error, axis=-1, keepdims=True)
-        gradient = (error * lax.rsqrt(spread + 1e-06)).astype(jnp.bfloat16)
-        gradients = lax.all_gather(gradient, ("tok", "lyr"), axis=0, tiled=True)
+    partial = jnp.dot(dense, weights, preferred_element_type=jnp.float32).astype(jnp.bfloat16)
+    rebuilt = lax.psum_scatter(partial, ("tok", "lyr"), scatter_dimension=0, tiled=True)
+    error = resid.astype(jnp.float32) - rebuilt.astype(jnp.float32)
+    spread = jnp.mean(error * error, axis=-1, keepdims=True)
+    gradient = (error * lax.rsqrt(spread + 1e-06)).astype(jnp.bfloat16)
+    gradients = lax.all_gather(gradient, ("tok", "lyr"), axis=0, tiled=True)
     projected = lax.dot_general(
         gradients, weights, (((1,), (1,)), ((), ())), preferred_element_type=jnp.float32
     ).astype(jnp.bfloat16)

time: 375 us -> 180 us (0.48)
  waiting for transfers between devices: 94.7 us -> 0 us
  local copies, waits for them, and re-layouts: 87.9 us -> 5.01 us
  Pallas kernels: 112 us -> 168 us
  matrix products: 24.8 us -> 0 us
  blocking collectives: 23.4 us -> 0 us
  other arithmetic: 17.1 us -> 3.54 us
  between operations: 14.1 us -> 0.68 us
    unnamed x3 -> x0, waiting for transfers between devices: 65.9 us -> none
    pallas_call x2, Pallas kernels: 112 us -> 168 us  [the longest x1 88.6 us: reduce_rows(): pl.pallas_call(reduce_kernel, out_shape=(jax.ShapeDtypeStruct(block, bf16...]
    unnamed x8 -> x2, local copies, waits for them, and re-layouts: 28.9 us -> 0.01 us
    all_gather x1 -> x0, waiting for transfers between devices: 28.8 us -> none  [per_device(): all_codes = lax.all_gather(masked, 'tok', axis=1, tiled=True)]
    dot_general x2 -> x0, matrix products: 24.8 us -> none  [the longest x1 18.5 us: per_device(): lax.dot_general(gradients, weights, (((1,), (1,)), ((), ())), preferred_e...]
    all_gather x1 -> x0, blocking collectives: 23.4 us -> none  [per_device(): numbers = lax.all_gather(numbers, 'tok', axis=1, tiled=True)]
    transpose x2 -> x1, local copies, waits for them, and re-layouts: 23.9 us -> 0.73 us  [per_device(): by_k = jnp.moveaxis(masked, 1, 2).reshape(layers_here * kact, count, panel)]
    reduce_sum x2 -> x0, other arithmetic: 9.47 us -> none  [the longest x1 5.54 us: per_device(): spread_out = jnp.sum(scored * jnp.swapaxes(named, 0, 1)[..., None], axis=3)]
  transfers between devices with their start and end apart: 2 -> 0, of which waited for: 2 -> 0; matrix products, arithmetic and copies ran while one was open for 2% -> 0% of each run, Pallas kernels for 0% -> 0%
where the time goes in v3:
time: 180 us; the launch traced here: 178 us
  Pallas kernels  168 us (93%)
  local copies, waits for them, and re-layouts  5.01 us (3%)
  other arithmetic  3.54 us (2%)
    pallas_call x1, Pallas kernels, reduce_rows(): pl.pallas_call(reduce_kernel, out_shape=(jax.ShapeDtypeStruct(block, bf16...  88.6 us
    pallas_call x1, Pallas kernels, gather_rows(): pl.pallas_call(gather_kernel, out_shape=(jax.ShapeDtypeStruct((4, 2 * row...  79.7 us

profile of v3, /device:TPU:0, one launch (start us, length us, event | category | flops | bytes accessed | tf_op | source)
XLA Modules:
  0.0 177.5 jit_solution(17441838772681832858)
XLA Ops:
  0.6 0.0 copy-start
  0.7 0.8 broadcast_compare_fusion
  1.4 0.1 pad.2.clone
  1.5 1.4 add_add_fusion.local_numbers_ref
  2.9 1.4 fusion
  4.3 0.7 copy.8
  5.0 0.0 copy-done
  5.0 0.7 constant_dynamic-slice_fusion.resid_ref
  5.8 88.6 %reduce_rows.1 = (bf16[64,2304]{1,0:T(8,128)(2,1)}, bf16[8,2,128,1024]{3,2,1,0:T(8,128)(2,1)}, s32[16,8,128]{2,1,0:T(8,128)}) custom-call(bf16[4,128,256]{2,1,0:T(8,128)(2,1)} %bitcast.14, s32[8,128]{1,0:T(8,128)} %add_add_fusion.local_numbers_ref, bf16[1024,2304]{1,0:T(8,128)(2,1)} %bitcast.12, bf16[64,2304]{1,0:T(8,128)(2,1)} %constant_dynamic-slice_fusion.resid_ref), custom_call_target="tpu_custom_call" | custom-call | tf_op jit(solution)/shard_map/reduce_rows/pallas_call | solution.py:458
  94.4 79.7 %gather_rows.1 = (bf16[4,128,256]{2,1,0:T(8,128)(2,1)}, f32[16,1024]{1,0:T(8,128)}) custom-call(bf16[64,2304]{1,0:T(8,128)(2,1)} %get-tuple-element.7.own_ref, bf16[8,2,128,1024]{3,2,1,0:T(8,128)(2,1)} %get-tuple-element.8.dense_ref, bf16[1024,2304]{1,0:T(8,128)(2,1)} %bitcast.13, s32[16,8,128]{2,1,0:T(8,128)} %get-tuple-element.9.numbers_ref, ...), custom_call_target="tpu_custom_call" | custom-call | tf_op jit(solution)/shard_map/gather_rows/pallas_call | solution.py:255
  174.1 1.9 %copy.11 = bf16[2,2,128,256]{3,1,2,0:T(2,128)(2,1)} copy(bf16[2,2,128,256]{3,2,1,0:T(8,128)(2,1)} %bitcast.16) | data formatting | bytes 524288 | tf_op jit(solution)/shard_map/reshape | solution.py:510
  176.0 1.5 reshape.53
  (2 shorter events, 0.0 us)
Async XLA Ops:
  0.6 4.4 %copy-start = (bf16[128,2304]{1,0:T(8,128)(2,1)S(1)}, bf16[128,2304]{1,0:T(8,128)(2,1)}, u32[]{:S(2)}) copy-start(bf16[128,2304]{1,0:T(8,128)(2,1)} %param.10) | copy-start | bytes 1769476

commit v4 on v3

--- a/solution.py
+++ b/solution.py
@@ -69,7 +69,7 @@
 
 
 def gather_kernel(
-    own_ref, dense_ref, weights_ref, numbers_ref, local_numbers_ref, scores_ref, totals_ref,
+    own_ref, dense_ref, weights_ref, numbers_ref, hot_ref, sent_ref, scores_ref, totals_ref,
     out_ref, slot_out, slot_in, local_sem, recv_sem, core_sem, first_sem, second_sem, z_sem, slot_send, slot_recv,
 ):
     at = Place()
@@ -168,8 +168,8 @@
                 totals_ref[:, cols] += jnp.dot(members[x], high, preferred_element_type=jnp.float32) + jnp.dot(
                     members[x], low, preferred_element_type=jnp.float32
                 )
-                held = slots(numbers[x], layer, at.tok * 2 + which, 1)
-                packed = jnp.dot(held[0] + held[1], high, preferred_element_type=jnp.float32).astype(jnp.bfloat16)
+                hot = hot_ref[sources[x], layer, which * CAP : (which + 1) * CAP, :]
+                packed = jnp.dot(hot, high, preferred_element_type=jnp.float32).astype(jnp.bfloat16)
                 slot_out[sources[x], layer, which * CAP : (which + 1) * CAP, :] = packed
         for x in (0, 1):
             if own:
@@ -216,11 +216,10 @@
             slot_out.at[0], slot_in.at[source], slot_send.at[0], slot_recv.at[source], at.to_core
         ).wait_recv()
     for layer in (0, 1):
-        held = slots(local_numbers_ref[...], layer, 0, 32)
         table = slot_in[:, layer].reshape(32 * CAP, panel)
         for k in (0, 1):
             scores_ref[2 * layer + k] = lax.dot_general(
-                held[k], table, (((0,), (0,)), ((), ())), preferred_element_type=jnp.float32
+                sent_ref[2 * layer + k], table, (((0,), (0,)), ((), ())), preferred_element_type=jnp.float32
             ).astype(scores_ref.dtype)
     for distance in range(1, 16):
         source = (at.tok + distance) % 16
@@ -248,7 +247,7 @@
             remote(own_ref, own_ref, z_sem.at[i], recv_sem.at[0], at.to_core).wait_send()
 
 
-def gather_rows(own, dense, weights, numbers, local_numbers, panel):
+def gather_rows(own, dense, weights, numbers, hot, sent, panel):
     rows, width = own.shape
     dma, bf16 = pltpu.SemaphoreType.DMA, jnp.bfloat16
     vmem = pl.BlockSpec(memory_space=pltpu.VMEM)
@@ -258,7 +257,7 @@
             jax.ShapeDtypeStruct((4, 2 * rows, panel), bf16),
             jax.ShapeDtypeStruct((REQUESTS, weights.shape[0]), jnp.float32),
         ),
-        in_specs=[vmem] * 5,
+        in_specs=[vmem] * 6,
         out_specs=(vmem, vmem),
         scratch_shapes=[
             pltpu.VMEM((32, rows, width), bf16),
@@ -270,11 +269,12 @@
             collective_id=1, has_side_effects=True, vmem_limit_bytes=60 * 1024 * 1024
         ),
         name="gather_rows",
-    )(own, dense, weights, numbers, local_numbers)
+    )(own, dense, weights, numbers, hot, sent)
 
 
 def reduce_kernel(
-    masked_ref, local_numbers_ref, weights_ref, resid_ref, out_ref, codes_ref, numbers_ref,
+    masked_ref, local_numbers_ref, weights_ref, resid_ref,
+    out_ref, codes_ref, numbers_ref, hot_ref, sent_ref,
     packed, slot_in, slot_send, slot_recv, number_send, number_recv, held, core_out, core_in, first_out, first_in, second_out, second_in, z_out, z_in,
     core_send, core_recv, first_send, first_recv, second_send, second_recv, z_send, z_recv,
 ):
@@ -283,54 +283,62 @@
     rows, width = out_ref.shape
     depth = codes_ref.shape[-1]
     panel = packed.shape[-1]
+    far = at.near[::-1]
     local = local_numbers_ref[...]
     numbers_ref[at.tok] = local
     for layer in (0, 1):
         sent = slots(local, layer, 0, 32)
+        for k in (0, 1):
+            sent_ref[2 * layer + k] = sent[k]
         value = sum(
             jnp.dot(sent[k], masked_ref[2 * layer + k], preferred_element_type=jnp.float32) for k in (0, 1)
         )
         packed[:, layer] = value.astype(packed.dtype).reshape(16, 2 * CAP, panel)
 
-    def slot_copies(distance):
-        target = (at.tok + distance) % 16
+    def peers(i):
+        return [far[i] * 4 + (at.tok + step) % 4 for step in range(1 if i == 3 else 0, 4)]
+
+    def slot_copies(target, source):
         return (
+            remote(packed.at[target], slot_in.at[source], slot_send.at[target], slot_recv.at[source], (target, at.y)),
             remote(
-                packed.at[target], slot_in.at[at.tok], slot_send.at[distance], slot_recv.at[distance], (target, at.y)
-            ),
-            remote(
-                local_numbers_ref, numbers_ref.at[at.tok], number_send.at[distance], number_recv.at[distance],
+                local_numbers_ref, numbers_ref.at[source], number_send.at[target], number_recv.at[source],
                 (target, at.y),
             ),
         )
 
-    for distance in range(1, 16):
-        for copy in slot_copies(distance):
-            copy.start()
+    for i in range(4):
+        for target in peers(i):
+            for copy in slot_copies(target, at.tok):
+                copy.start()
     slot_in[at.tok] = packed[at.tok]
-    for distance in range(1, 16):
-        for copy in slot_copies(distance):
-            copy.wait_recv()
-
-    @pl.loop(0, 16)
-    def _(source):
-        for layer in (0, 1):
-            held_slots = slots(numbers_ref[source], layer, at.tok * 2, 2)
-            hot = held_slots[0] + held_slots[1]
-            for which in (0, 1):
-                part = slice(which * CAP, (which + 1) * CAP)
-                n = 2 * layer + which
-                codes_ref[(source // 4) * 2 + source % 2, (source // 2) % 2, :, n * panel : (n + 1) * panel] = (
-                    lax.dot_general(
-                        hot[part], slot_in[source, layer, part, :], (((0,), (0,)), ((), ())),
-                        preferred_element_type=jnp.float32,
-                    ).astype(codes_ref.dtype)
-                )
+
+    def unpack(i):
+        for source in peers(i):
+            for copy in slot_copies(source, source):
+                copy.wait_recv()
+
+        @pl.loop(0, 4)
+        def _(step):
+            source = far[i] * 4 + step
+            for layer in (0, 1):
+                held_slots = slots(numbers_ref[source], layer, at.tok * 2, 2)
+                hot = held_slots[0] + held_slots[1]
+                hot_ref[source, layer] = hot
+                for which in (0, 1):
+                    part = slice(which * CAP, (which + 1) * CAP)
+                    n = 2 * layer + which
+                    codes_ref[far[i] * 2 + step % 2, step // 2, :, n * panel : (n + 1) * panel] = (
+                        lax.dot_general(
+                            hot[part], slot_in[source, layer, part, :], (((0,), (0,)), ((), ())),
+                            preferred_element_type=jnp.float32,
+                        ).astype(codes_ref.dtype)
+                    )
 
     tile = 256 if width % 256 == 0 else width
-    far = at.near[::-1]
 
     def product(i):
+        unpack(i)
         for core in (1 - at.c, at.c):
             left = codes_ref[far[i] * 2 + core].reshape(4 * rows, depth)
             away = core is not at.c
@@ -436,9 +444,10 @@
     over_second(3)
     along_z(2)
     along_z(3)
-    for distance in range(1, 16):
-        for copy in slot_copies(distance):
-            copy.wait_send()
+    for i in range(4):
+        for target in peers(i):
+            for copy in slot_copies(target, target):
+                copy.wait_send()
     for i in range(4):
         core_copy(i).wait_send()
         first_copy(i, 0).wait_send()
@@ -461,9 +470,11 @@
             jax.ShapeDtypeStruct(block, bf16),
             jax.ShapeDtypeStruct((8, 2, 2 * rows, depth), bf16),
             jax.ShapeDtypeStruct((16,) + local_numbers.shape, jnp.int32),
+            jax.ShapeDtypeStruct((16, 2, 2 * CAP, 2 * rows), bf16),
+            jax.ShapeDtypeStruct((4, 32 * CAP, 2 * rows), bf16),
         ),
         in_specs=[vmem] * 4,
-        out_specs=(vmem,) * 3,
+        out_specs=(vmem,) * 5,
         scratch_shapes=[
             pltpu.VMEM((16, 2, 2 * CAP, panel), bf16),
             pltpu.VMEM((16, 2, 2 * CAP, panel), bf16),
@@ -505,8 +516,9 @@
     if grid:
         numbers = jnp.concatenate([numbers, jnp.zeros((8 - numbers.shape[0], count), jnp.int32)], axis=0)
         by_k = jnp.moveaxis(masked, 1, 2).reshape(layers_here * kact, count, panel)
-        gradient, dense, all_numbers = reduce_rows(by_k, numbers, weights, resid)
-        scores, totals = gather_rows(gradient, dense, weights, all_numbers, numbers, panel)
+        gradient, *rest = reduce_rows(by_k, numbers, weights, resid)
+        dense, all_numbers, hot, sent = rest
+        scores, totals = gather_rows(gradient, dense, weights, all_numbers, hot, sent, panel)
         scores = jnp.moveaxis(scores.reshape(layers_here, kact, count, panel), 1, 2)
         return (scores, totals.reshape(REQUESTS, layers_here, features))
     all_codes = lax.all_gather(masked, "tok", axis=1, tiled=True)

time: 180 us -> 166 us (0.922)
  Pallas kernels: 168 us -> 156 us
    pallas_call x1, Pallas kernels: 88.6 us -> 80.6 us  [reduce_rows(): pl.pallas_call(reduce_kernel, out_shape=(jax.ShapeDtypeStruct(block, bf16...]
    pallas_call x1, Pallas kernels: 79.7 us -> 75 us  [gather_rows(): pl.pallas_call(gather_kernel, out_shape=(jax.ShapeDtypeStruct((4, 2 * row...]
where the time goes in v4:
time: 166 us; the launch traced here: 165 us
  Pallas kernels  156 us (94%)
  local copies, waits for them, and re-layouts  5.01 us (3%)
  other arithmetic  3.54 us (2%)
    pallas_call x1, Pallas kernels, reduce_rows(): pl.pallas_call(reduce_kernel, out_shape=(jax.ShapeDtypeStruct(block, bf16...  80.6 us
    pallas_call x1, Pallas kernels, gather_rows(): pl.pallas_call(gather_kernel, out_shape=(jax.ShapeDtypeStruct((4, 2 * row...  75 us

profile of v4, /device:TPU:0, one launch (start us, length us, event | category | flops | bytes accessed | tf_op | source)
XLA Modules:
  0.0 164.8 jit_solution(6171105397708266686)
XLA Ops:
  0.6 0.0 copy-start
  0.7 0.8 broadcast_compare_fusion
  1.4 0.1 pad.2.clone
  1.5 1.4 add_add_fusion.local_numbers_ref
  2.9 1.4 fusion
  4.3 0.7 copy.8
  5.0 0.0 copy-done
  5.0 0.7 constant_dynamic-slice_fusion.resid_ref
  5.8 80.6 %reduce_rows.1 = (bf16[64,2304]{1,0:T(8,128)(2,1)}, bf16[8,2,128,1024]{3,2,1,0:T(8,128)(2,1)}, s32[16,8,128]{2,1,0:T(8,128)}, bf16[16,2,32,128]{3,2,1,0:T(8,128)(2,1)}, bf16[4,512,128]{2,1,0:T(8,128)(2,1)}) custom-call(bf16[4,128,256]{2,1,0:T(8,128)(2,1)} %bitcast.14, s32[8,128]{1,0:T(8,128)} %add_add_fusion.local_numbers_ref, bf16[1024,2304]{1,0:T(8,128)(2,1)} %bitcast.12, ...), custom_call_target="tpu_custom_call" | custom-call | tf_op jit(solution)/shard_map/reduce_rows/pallas_call | solution.py:467
  86.3 75.0 %gather_rows.1 = (bf16[4,128,256]{2,1,0:T(8,128)(2,1)}, f32[16,1024]{1,0:T(8,128)}) custom-call(bf16[64,2304]{1,0:T(8,128)(2,1)} %get-tuple-element.9.own_ref, bf16[8,2,128,1024]{3,2,1,0:T(8,128)(2,1)} %get-tuple-element.10.dense_ref, bf16[1024,2304]{1,0:T(8,128)(2,1)} %bitcast.13, s32[16,8,128]{2,1,0:T(8,128)} %get-tuple-element.11.numbers_ref, ...), custom_call_target="tpu_custom_call" | custom-call | tf_op jit(solution)/shard_map/gather_rows/pallas_call | solution.py:254
  161.3 1.9 %copy.11 = bf16[2,2,128,256]{3,1,2,0:T(2,128)(2,1)} copy(bf16[2,2,128,256]{3,2,1,0:T(8,128)(2,1)} %bitcast.16) | data formatting | bytes 524288 | tf_op jit(solution)/shard_map/reshape | solution.py:522
  163.3 1.5 reshape.53
  (2 shorter events, 0.0 us)
Async XLA Ops:
  0.6 4.4 %copy-start = (bf16[128,2304]{1,0:T(8,128)(2,1)S(1)}, bf16[128,2304]{1,0:T(8,128)(2,1)}, u32[]{:S(2)}) copy-start(bf16[128,2304]{1,0:T(8,128)(2,1)} %param.10) | copy-start | bytes 1769476

commit v5 on v4

--- a/solution.py
+++ b/solution.py
@@ -196,9 +196,9 @@
     from_second(2)
     from_z(3)
     from_first(1, True)
-    project(at.near[0], at.c, True)
     from_first(2, False)
     from_second(3)
+    project(at.near[0], at.c, True)
     from_core(0)
     project(at.near[1], at.c, False)
     from_first(2, True)
@@ -429,15 +429,15 @@
             out_ref[...] = (error * lax.rsqrt(spread + 1e-06)).astype(out_ref.dtype)
 
     product(0)
+    over_first(0)
     product(1)
-    over_first(0)
-    product(2)
     over_first(1)
     over_second(0)
-    product(3)
+    product(2)
     over_first(2)
     over_second(1)
     along_z(0)
+    product(3)
     over_first(3)
     over_second(2)
     along_z(1)

time: 166 us -> 164 us (0.988)
  Pallas kernels: 156 us -> 154 us
    pallas_call x1, Pallas kernels: 80.6 us -> 75.8 us  [reduce_rows(): pl.pallas_call(reduce_kernel, out_shape=(jax.ShapeDtypeStruct(block, bf16...]
    pallas_call x1, Pallas kernels: 75 us -> 78.1 us  [gather_rows(): pl.pallas_call(gather_kernel, out_shape=(jax.ShapeDtypeStruct((4, 2 * row...]
where the time goes in v5:
time: 164 us; the launch traced here: 163 us
  Pallas kernels  154 us (94%)
  local copies, waits for them, and re-layouts  5.01 us (3%)
  other arithmetic  3.54 us (2%)
    pallas_call x1, Pallas kernels, gather_rows(): pl.pallas_call(gather_kernel, out_shape=(jax.ShapeDtypeStruct((4, 2 * row...  78.1 us
    pallas_call x1, Pallas kernels, reduce_rows(): pl.pallas_call(reduce_kernel, out_shape=(jax.ShapeDtypeStruct(block, bf16...  75.8 us

profile of v5, /device:TPU:0, one launch (start us, length us, event | category | flops | bytes accessed | tf_op | source)
XLA Modules:
  0.0 163.2 jit_solution(4595222512565337545)
XLA Ops:
  0.6 0.0 copy-start
  0.7 0.8 broadcast_compare_fusion
  1.4 0.1 pad.2.clone
  1.5 1.4 add_add_fusion.local_numbers_ref
  2.9 1.4 fusion
  4.3 0.7 copy.8
  5.0 0.0 copy-done
  5.0 0.7 constant_dynamic-slice_fusion.resid_ref
  5.8 75.8 %reduce_rows.1 = (bf16[64,2304]{1,0:T(8,128)(2,1)}, bf16[8,2,128,1024]{3,2,1,0:T(8,128)(2,1)}, s32[16,8,128]{2,1,0:T(8,128)}, bf16[16,2,32,128]{3,2,1,0:T(8,128)(2,1)}, bf16[4,512,128]{2,1,0:T(8,128)(2,1)}) custom-call(bf16[4,128,256]{2,1,0:T(8,128)(2,1)} %bitcast.14, s32[8,128]{1,0:T(8,128)} %add_add_fusion.local_numbers_ref, bf16[1024,2304]{1,0:T(8,128)(2,1)} %bitcast.12, ...), custom_call_target="tpu_custom_call" | custom-call | tf_op jit(solution)/shard_map/reduce_rows/pallas_call | solution.py:467
  81.6 78.1 %gather_rows.1 = (bf16[4,128,256]{2,1,0:T(8,128)(2,1)}, f32[16,1024]{1,0:T(8,128)}) custom-call(bf16[64,2304]{1,0:T(8,128)(2,1)} %get-tuple-element.9.own_ref, bf16[8,2,128,1024]{3,2,1,0:T(8,128)(2,1)} %get-tuple-element.10.dense_ref, bf16[1024,2304]{1,0:T(8,128)(2,1)} %bitcast.13, s32[16,8,128]{2,1,0:T(8,128)} %get-tuple-element.11.numbers_ref, ...), custom_call_target="tpu_custom_call" | custom-call | tf_op jit(solution)/shard_map/gather_rows/pallas_call | solution.py:254
  159.7 1.9 %copy.11 = bf16[2,2,128,256]{3,1,2,0:T(2,128)(2,1)} copy(bf16[2,2,128,256]{3,2,1,0:T(8,128)(2,1)} %bitcast.16) | data formatting | bytes 524288 | tf_op jit(solution)/shard_map/reshape | solution.py:522
  161.6 1.5 reshape.53
  (2 shorter events, 0.0 us)
Async XLA Ops:
  0.6 4.4 %copy-start = (bf16[128,2304]{1,0:T(8,128)(2,1)S(1)}, bf16[128,2304]{1,0:T(8,128)(2,1)}, u32[]{:S(2)}) copy-start(bf16[128,2304]{1,0:T(8,128)(2,1)} %param.10) | copy-start | bytes 1769476
